TPU v7x, 128 devices: a whole 4x4x4 slice. The times are simulated.
128 devices in a mesh: shaft: 16 (over y, z), lat: 8 (over x, core).
Axes of the slice: x: 4, y: 4, z: 4, core: 2. Of those that a mesh axis runs over, the one named last changes fastest.
Arguments:
- sphere_position: float32 [3, 16, 16, 8, 128], P(None, 'shaft', 'lat'), may hold values from 0 to 5
- sphere_velocity: float32 [3, 16, 16, 8, 128], P(None, 'shaft', 'lat'), may hold values from -6 to 6
- sphere_radius: float32 [16, 16, 8, 128], P('shaft', 'lat'), may hold values from 0.4 to 0.6
- sphere_offset: float32 [3, 16, 16, 8, 128], P(None, 'shaft', 'lat'), may hold values from -6 to 6
- sphere_piece: int32 [16, 8, 2048], P('shaft', 'lat'), may hold values from 0 to 511, never falling along the last dimension, each value on 1 to 64 neighbouring positions
- piece_route: int32 [16, 8, 512], P('shaft', 'lat'), may hold values from 0 to 8, as said below
- piece_clump: int32 [16, 8, 512], P('shaft', 'lat'), may hold values from 0 to 255
- blade_phase: int32 [1], replicated, may hold values from 0 to 63
- clump_centre: float32 [3, 16, 8, 256], P(None, 'shaft', 'lat'), may hold values from -6 to 6
- clump_motion: float32 [6, 16, 8, 256], P(None, 'shaft', 'lat'), may hold values from -6 to 6
- clump_angles: float32 [3, 16, 8, 256], P(None, 'shaft', 'lat'), may hold values from -3.140625 to 3.140625
- clump_inverse_mass: float32 [16, 8, 256], P('shaft', 'lat'), may hold values from 0.05 to 0.5
- clump_inverse_inertia: float32 [3, 16, 8, 256], P(None, 'shaft', 'lat'), may hold values from 0.01 to 0.1
Outputs:
- clump_next: float32 [9, 16, 8, 256], P(None, 'shaft', 'lat')
- sphere_next: float32 [6, 16, 16, 8, 128], P(None, 'shaft', 'lat')
Inputs may be any that keep to these rules, and one draw needn't show every extreme that they name: `sphere_piece`: each device's spheres, in the order of the steps, form 512 runs of consecutive spheres numbered in order, each of 1 to 64 spheres; some run has exactly 64. `piece_route`: a code never names a lateral index outside the slabs; on every device no code is named by more than 128 pieces, and one code exactly 128 times.
All inputs are finite; a program needn't handle non-finite values.
Results may differ from a plain program's by a relative error of at most 0.0003.
Values sent between devices are 32-bit elements; how exact they have to be, the bound alone decides.
A program may use at most 128 MiB of HBM per device.

v0:
```python
import math

import jax
import jax.numpy as jnp
from jax import lax
from jax.sharding import PartitionSpec as P

PHASES = 64


CELL_SIDE = 5.0
STIFFNESS = 10.0
NORMAL_DAMPING = 2.0
SHEAR_DAMPING = 2.0
COHESION = 0.5
FRICTION = 0.5
BLADE_STIFFNESS = 20.0
BLADE_THICKNESS = 1.0
TIME_STEP = 0.5
GRAVITY = 0.5


def with_halo(x, sides, width, wrap):
    for axis, dim in sides:
        peers, length = (lax.axis_size(axis), x.shape[dim])
        up = [(i, (i + 1) % peers) for i in range(peers if wrap else peers - 1)]
        down = [(j, i) for i, j in up]
        last = lax.slice_in_dim(x, length - width, length, axis=dim)
        initial = lax.slice_in_dim(x, 0, width, axis=dim)
        before = lax.ppermute(last, axis, up)
        after = lax.ppermute(initial, axis, down)
        x = jnp.concatenate([before, x, after], axis=dim)
    return x


def shifted_2(value, axis, steps):
    count = lax.axis_size(axis)
    pairs = [(source, (source + steps) % count) for source in range(count)]
    return lax.ppermute(value, axis, pairs)


def shifted_3(x, axis, by):
    peers = lax.axis_size(axis)
    pairs = [(i, i + by) for i in range(peers) if 0 <= i + by < peers]
    return lax.ppermute(x, axis, pairs)


def offsets(tile_kind):
    packed = tile_kind + (tile_kind >= 13).astype(jnp.int32)
    return (packed // 9 - 1, packed // 3 % 3 - 1, packed % 3 - 1)


def cross_product(left, right):
    return jnp.stack(
        [
            left[1] * right[2] - left[2] * right[1],
            left[2] * right[0] - left[0] * right[2],
            left[0] * right[1] - left[1] * right[0],
        ],
        0,
    )


def pair_force(
    position_mine,
    velocity_mine,
    radius_mine,
    position_other,
    velocity_other,
    radius_other,
    keep_mask,
):
    separation = position_mine[:, :, :, None] - position_other[:, :, None, :]
    radius_sum = radius_mine[:, :, None] + radius_other[:, None, :]
    distance = jnp.sqrt(jnp.sum(separation * separation, 0))
    distance = jnp.maximum(distance, 0.25 * radius_sum)
    normal = separation / distance
    intersection = jnp.maximum(radius_sum - distance, 0.0)
    reduced = radius_mine[:, :, None] * radius_other[:, None, :] / radius_sum
    stiff_root = jnp.sqrt(reduced * intersection)
    relative = velocity_mine[:, :, :, None] - velocity_other[:, :, None, :]
    normal_speed = jnp.sum(relative * normal, 0)
    sliding = relative - normal_speed * normal
    normal_force = stiff_root * (
        STIFFNESS * intersection - NORMAL_DAMPING * normal_speed - COHESION
    )
    friction_cap = FRICTION * STIFFNESS * stiff_root * intersection
    shear_force = -SHEAR_DAMPING * stiff_root * sliding
    factor = friction_cap / jnp.sqrt(
        jnp.sum(shear_force * shear_force, 0) + friction_cap * friction_cap + 1e-06
    )
    forces = (normal_force * normal + factor * shear_force) * keep_mask
    return jnp.sum(forces, 3)


def tile_forces(source, mine, targets, shifts):
    tile_rows, per_cell = targets.shape
    cell_size = mine.shape[2]
    joined = tile_rows * per_cell
    others = jnp.take(source, targets.reshape(-1), axis=1)
    repeated = jnp.broadcast_to(mine[:, :, None, :], (7, tile_rows, per_cell, cell_size)).reshape(
        7, joined, cell_size
    )
    shifted = others[0:3] + shifts.reshape(3, joined)[:, :, None]
    first_kind = (jnp.arange(joined) % per_cell == 0).astype(jnp.float32)
    identity = jnp.eye(cell_size, dtype=jnp.float32)
    keep_mask = 1.0 - first_kind[:, None, None] * identity[None]
    forces = pair_force(
        repeated[0:3], repeated[3:6], repeated[6], shifted, others[3:6], others[6], keep_mask
    )
    return jnp.sum(forces.reshape(3, tile_rows, per_cell, cell_size), 2)


def tile_lists(shaft_cell, lateral_cell, upward_cell, lat_cells, height_cells):
    cell_codes = jnp.broadcast_to(
        jnp.arange(26, dtype=jnp.int32)[None, :], (shaft_cell.shape[0], 26)
    )
    step_shaft, step_lat, step_up = offsets(cell_codes)
    zero_col = jnp.zeros_like(cell_codes[:, :1])
    step_shaft = jnp.concatenate([zero_col, step_shaft], 1)
    step_lat = jnp.concatenate([zero_col, step_lat], 1)
    step_up = jnp.concatenate([zero_col, step_up], 1)
    targets = (
        (
            (shaft_cell[:, None] + 1 + step_shaft) * (lat_cells + 2)
            + lateral_cell[:, None]
            + 1
            + step_lat
        )
        * (height_cells + 2)
        + upward_cell[:, None]
        + 1
        + step_up
    )
    shifts = CELL_SIDE * jnp.stack([step_shaft, step_lat, step_up], 0).astype(jnp.float32)
    return (targets, shifts)


def blade_force(
    position,
    radius,
    shaft_cell,
    lateral_cell,
    upward_cell,
    blade_phase,
    lat_cells,
    height_cells,
    shaft_per_device,
):
    global_x = CELL_SIDE * shaft_cell.astype(jnp.float32) + position[0]
    global_y = CELL_SIDE * lateral_cell.astype(jnp.float32) + position[1]
    global_z = CELL_SIDE * upward_cell.astype(jnp.float32) + position[2]
    blade_angle = blade_phase[0].astype(jnp.float32) * (2.0 * math.pi / PHASES)
    blade_cos = jnp.cos(blade_angle)
    blade_sin = jnp.sin(blade_angle)
    centre_y = 0.5 * CELL_SIDE * lat_cells
    centre_z = 0.5 * CELL_SIDE * height_cells
    blade_reach = 0.45 * CELL_SIDE * min(lat_cells, height_cells)
    across = (global_y - centre_y) * blade_cos + (global_z - centre_z) * blade_sin
    radial = (global_z - centre_z) * blade_cos - (global_y - centre_y) * blade_sin
    contact_depth = jnp.maximum(
        jnp.minimum(radius - across, radius + BLADE_THICKNESS + across), 0.0
    )
    window = jnp.maximum(radial * (blade_reach - radial), 0.0) * (4.0 / (blade_reach * blade_reach))
    strip_gate = jnp.maximum(
        jnp.cos(global_x * (2.0 * math.pi / (2.0 * CELL_SIDE * shaft_per_device))), 0.0
    )
    magnitude = BLADE_STIFFNESS * contact_depth * window * strip_gate
    return jnp.stack([jnp.zeros_like(magnitude), magnitude * blade_cos, magnitude * blade_sin], 0)


def rigid_update(sums, centre, motion, angles, inverse_mass, inverse_inertia):
    gravity_vec = jnp.array([0.0, 0.0, -GRAVITY], dtype=jnp.float32)[:, None]
    velocity = motion[0:3] + TIME_STEP * (inverse_mass[None] * sums[0:3] + gravity_vec)
    cos_z, sin_z = (jnp.cos(angles[0]), jnp.sin(angles[0]))
    cos_y, sin_y = (jnp.cos(angles[1]), jnp.sin(angles[1]))
    cos_x, sin_x = (jnp.cos(angles[2]), jnp.sin(angles[2]))
    rotation = [
        [
            cos_z * cos_y,
            cos_z * sin_y * sin_x - sin_z * cos_x,
            cos_z * sin_y * cos_x + sin_z * sin_x,
        ],
        [
            sin_z * cos_y,
            sin_z * sin_y * sin_x + cos_z * cos_x,
            sin_z * sin_y * cos_x - cos_z * sin_x,
        ],
        [-sin_y, cos_y * sin_x, cos_y * cos_x],
    ]
    torque = sums[3:6]
    body_torque = [
        sum((rotation[row_index][col_index] * torque[row_index] for row_index in range(3)))
        for col_index in range(3)
    ]
    scaled = [inverse_inertia[col_index] * body_torque[col_index] for col_index in range(3)]
    world = jnp.stack(
        [
            sum((rotation[row_index][col_index] * scaled[col_index] for col_index in range(3)))
            for row_index in range(3)
        ],
        0,
    )
    spin = motion[3:6] + TIME_STEP * world
    centre_next = centre + TIME_STEP * velocity
    return (centre_next, velocity, spin)


def turn_matrix(spin):
    half_turn = 0.5 * TIME_STEP * spin
    squared = jnp.sum(half_turn * half_turn, 0)
    scale = 2.0 / (1.0 + squared)
    skew_part = [
        [0.0, -half_turn[2], half_turn[1]],
        [half_turn[2], 0.0, -half_turn[0]],
        [-half_turn[1], half_turn[0], 0.0],
    ]
    entries = []
    for row_index in range(3):
        for col_index in range(3):
            entry_value = (
                skew_part[row_index][col_index] + half_turn[row_index] * half_turn[col_index]
            )
            if row_index == col_index:
                entry_value = 1.0 + scale * (entry_value - squared)
            else:
                entry_value = scale * entry_value
            entries.append(entry_value)
    return jnp.stack(entries, 0)


def on_device(
    sphere_position,
    sphere_velocity,
    sphere_radius,
    sphere_offset,
    sphere_piece,
    piece_route,
    piece_clump,
    blade_phase,
    clump_centre,
    clump_motion,
    clump_angles,
    clump_inverse_mass,
    clump_inverse_inertia,
):
    shaft_cells, lat_cells, height_cells, cell_size = sphere_radius.shape
    lat_count = lax.axis_size("lat")
    sphere_state = jnp.concatenate([sphere_position, sphere_velocity, sphere_radius[None]], 0)
    widened = with_halo(sphere_state, (("shaft", 1),), 1, True)
    extended = with_halo(widened, (("lat", 2),), 1, False)
    extended = jnp.pad(extended, ((0, 0), (0, 0), (0, 0), (1, 1), (0, 0)))
    source = extended.reshape(7, -1, cell_size)
    cell_total = shaft_cells * lat_cells * height_cells
    own_cells = sphere_state.reshape(7, cell_total, cell_size)
    batch_cells = min(4, cell_total)

    def cell_block(cell_ids):
        shaft_cell = cell_ids // (lat_cells * height_cells)
        lateral_cell = cell_ids // height_cells % lat_cells
        upward_cell = cell_ids % height_cells
        targets, shifts = tile_lists(shaft_cell, lateral_cell, upward_cell, lat_cells, height_cells)
        return tile_forces(source, own_cells[:, cell_ids], targets, shifts)

    contact = lax.map(cell_block, jnp.arange(cell_total, dtype=jnp.int32).reshape(-1, batch_cells))
    contact = jnp.transpose(contact, (1, 0, 2, 3)).reshape(
        3, shaft_cells, lat_cells, height_cells, cell_size
    )
    grid_shape = (shaft_cells, lat_cells, height_cells, cell_size)
    shaft_ids = (
        lax.broadcasted_iota(jnp.int32, grid_shape, 0) + lax.axis_index("shaft") * shaft_cells
    )
    lat_ids = lax.broadcasted_iota(jnp.int32, grid_shape, 1) + lax.axis_index("lat") * lat_cells
    height_ids = lax.broadcasted_iota(jnp.int32, grid_shape, 2)
    blade = blade_force(
        sphere_position,
        sphere_radius,
        shaft_ids,
        lat_ids,
        height_ids,
        blade_phase,
        lat_cells * lat_count,
        height_cells,
        shaft_cells,
    )
    sphere_force = contact + blade
    moment = cross_product(sphere_offset, sphere_force)
    sphere_total = cell_total * cell_size
    terms = jnp.concatenate([sphere_force, moment], 0).reshape(6, sphere_total)
    piece_ids = sphere_piece.reshape(sphere_total)
    piece_count = piece_route.shape[2]
    piece_sums = jax.ops.segment_sum(
        terms.T, piece_ids, num_segments=piece_count, indices_are_sorted=True
    )
    clump_count = clump_inverse_mass.shape[2]
    codes = piece_route.reshape(piece_count)
    clump_ids = piece_clump.reshape(piece_count)
    capacity = 16 * ((piece_count + 71) // 72)
    hits = (codes[:, None] == jnp.arange(9, dtype=jnp.int32)[None, :]).astype(jnp.int32)
    slots = jnp.sum((jnp.cumsum(hits, 0) - 1) * hits, 1)
    send_sums = jnp.zeros((9, capacity, 6), jnp.float32).at[codes, slots].set(piece_sums)
    send_ids = jnp.full((9, capacity), clump_count, jnp.int32).at[codes, slots].set(clump_ids)
    grid_sums = send_sums.reshape(3, 3, capacity, 6)
    grid_ids = send_ids.reshape(3, 3, capacity)
    shaft_sums = []
    shaft_ids_list = []
    for offset in (-1, 0, 1):
        if offset == 0:
            moved_sums, moved_ids = (grid_sums[1], grid_ids[1])
        else:
            moved_sums, moved_ids = shifted_2(
                (grid_sums[offset + 1], grid_ids[offset + 1]), "shaft", offset
            )
        shaft_sums.append(moved_sums)
        shaft_ids_list.append(moved_ids)
    section_sums = jnp.stack(shaft_sums, 0)
    section_ids = jnp.stack(shaft_ids_list, 0)
    lat_sums = []
    lat_ids_list = []
    for offset in (-1, 0, 1):
        if offset == 0:
            moved_sums, moved_ids = (section_sums[:, 1], section_ids[:, 1])
        else:
            moved_sums, moved_ids = shifted_3(
                (section_sums[:, offset + 1], section_ids[:, offset + 1]), "lat", offset
            )
        lat_sums.append(moved_sums)
        lat_ids_list.append(moved_ids)
    got_sums = jnp.stack(lat_sums, 1)
    got_ids = jnp.stack(lat_ids_list, 1)
    clump_sums = jax.ops.segment_sum(
        got_sums.reshape(-1, 6), got_ids.reshape(-1), num_segments=clump_count + 1
    )[:clump_count].T
    centre_next, velocity, spin = rigid_update(
        clump_sums,
        clump_centre.reshape(3, clump_count),
        clump_motion.reshape(6, clump_count),
        clump_angles.reshape(3, clump_count),
        clump_inverse_mass.reshape(clump_count),
        clump_inverse_inertia.reshape(3, clump_count),
    )
    motion_table = jnp.concatenate([velocity, spin, turn_matrix(spin)], 0)
    reply = jnp.take(motion_table.T, jnp.minimum(got_ids, clump_count - 1), axis=0)
    width = reply.shape[-1]
    lat_back = []
    for offset in (-1, 0, 1):
        if offset == 0:
            moved = reply[:, 1]
        else:
            moved = shifted_3(reply[:, offset + 1], "lat", -offset)
        lat_back.append(moved)
    section_back = jnp.stack(lat_back, 1)
    shaft_back = []
    for offset in (-1, 0, 1):
        if offset == 0:
            moved = section_back[1]
        else:
            moved = shifted_2(section_back[offset + 1], "shaft", -offset)
        shaft_back.append(moved)
    back_rows = jnp.stack(shaft_back, 0).reshape(9, capacity, width)
    piece_pose = back_rows[codes, slots]
    sphere_pose = jnp.take(piece_pose, piece_ids, axis=0).T
    offset_flat = sphere_offset.reshape(3, sphere_total)
    turned = jnp.stack(
        [
            sum(
                (
                    sphere_pose[6 + 3 * row_index + col_index] * offset_flat[col_index]
                    for col_index in range(3)
                )
            )
            for row_index in range(3)
        ],
        0,
    )
    moving = sphere_pose[0:3] + cross_product(sphere_pose[3:6], turned)
    sphere_next = jnp.concatenate([turned, moving], 0).reshape(
        6, shaft_cells, lat_cells, height_cells, cell_size
    )
    clump_next = jnp.concatenate([centre_next, velocity, spin], 0).reshape(9, 1, 1, clump_count)
    return (clump_next, sphere_next)


def solution(mesh):
    placed = (
        P(None, "shaft", "lat", None, None),
        P(None, "shaft", "lat", None, None),
        P("shaft", "lat", None, None),
        P(None, "shaft", "lat", None, None),
        P("shaft", "lat", None),
        P("shaft", "lat", None),
        P("shaft", "lat", None),
        P(),
        P(None, "shaft", "lat", None),
        P(None, "shaft", "lat", None),
        P(None, "shaft", "lat", None),
        P("shaft", "lat", None),
        P(None, "shaft", "lat", None),
    )
    return jax.shard_map(
        on_device,
        mesh=mesh,
        in_specs=placed,
        out_specs=(P(None, "shaft", "lat", None), P(None, "shaft", "lat", None, None)),
        check_vma=False,
    )
```

profile of v0, /device:TPU:1, one launch (start us, length us, event | category | flops | bytes accessed | tf_op | source)
XLA Modules:
  0.0 626.4 jit_solution(8931042346189398953)
XLA Ops:
  12.7 43.1 %scatter_fusion = s32[9,128]{1,0:T(8,128)S(1)} fusion(s32[9,128]{1,0:T(8,128)S(1)} %broadcast_in_dim.123, s32[512]{0:T(512)S(1)} %bitcast.419, s32[512]{0:T(512)} %bitcast.485), kind=kCustom, calls=%fused_computation.5 | custom fusion | bytes 10240 | tf_op jit(solution)/shard_map/scatter | solution.py:302
  85.4 440.0 %while.13 = (s32[]{:T(128)}, f32[4,3,4,128]{3,2,1,0:T(4,128)}, s32[4,4]{1,0:T(4,128)S(1)}, f32[7,16,128]{2,0,1:T(8,128)S(1)}, f32[7,120,128]{2,0,1:T(8,128)S(1)}, /*index=5*/s32[]{:T(128)}, f32[]{:T(128)}) while((s32[]{:T(128)}, f32[4,3,4,128]{3,2,1,0:T(4,128)}, s32[4,4]{1,0:T(4,128)S(1)}, f32[7,16,128]{2,0,1:T(8,128)S(1)}, ...), condition=%wide.region_10.11_spmd, body=%wide.region_4.10_spmd.sunk | while | flops 196589744 | bytes 224749776 | solution.py:265
  88.1 9.8 %fusion.82 = f32[108,128,128]{2,1,0:T(8,128)} fusion(f32[3,108,128]{2,1,0:T(8,128)S(1)} %copy.572, f32[3,108,128]{2,1,0:T(8,128)S(1)} %sub.459), kind=kLoop, calls=%fused_computation.13.clone.1 | loop fusion | flops 14155776 | bytes 7409664 | tf_op jit(solution)/shard_map/while/body/eval_jaxpr/reduce_sum | solution.py:75
  98.0 7.6 %fusion.83 = f32[108,128,128]{2,1,0:T(8,128)} fusion(f32[108,128,128]{2,1,0:T(8,128)} %fusion.82, f32[108,128]{1,0:T(8,128)S(1)} %bitcast.422, f32[108,128]{1,0:T(8,128)S(1)} %broadcast_in_dim.173), kind=kLoop, calls=%fused_computation.23.clone.4 | loop fusion | flops 5308416 | bytes 14266368 | tf_op jit(solution)/shard_map/while/body/eval_jaxpr/max | solution.py:76
  108.1 18.8 %fusion.84 = f32[108,128,128]{2,1,0:T(8,128)} fusion(f32[108,128,128]{2,1,0:T(8,128)} %fusion.83, f32[3,108,128]{2,1,0:T(8,128)S(1)} %copy.575, f32[3,108,128]{2,1,0:T(8,128)} %sub.460, f32[3,108,128]{2,1,0:T(8,128)S(1)} %copy.572, f32[3,108,128]{2,1,0:T(8,128)S(1)} %sub.459), kind=kLoop, calls=%fused_computation.14.clone.1 | loop fusion | flops 24772608 | bytes 14819328 | tf_op jit(solution)/shard_map/while/body/eval_jaxpr/reduce_sum | solution.py:82
  126.9 11.4 %add_multiply_fusion.9 = (f32[108,128,128]{2,1,0:T(8,128)}, f32[108,128,128]{2,1,0:T(8,128)}) fusion(f32[108,128,128]{2,1,0:T(8,128)} %fusion.84, f32[108,128]{1,0:T(8,128)S(1)} %bitcast.423, f32[108,128]{1,0:T(8,128)S(1)} %broadcast_in_dim.173, f32[108,128,128]{2,1,0:T(8,128)S(1)} %bitcast.418), kind=kLoop, calls=%fused_computation.27.clone.1 | loop fusion | flops 24772608 | bytes 28422144 | tf_op jit(solution)/shard_map/while/body/eval_jaxpr/mul | solution.py:84
  138.3 19.0 %multiply_reduce_fusion.5 = f32[108,128,128]{2,1,0:T(8,128)} fusion(f32[108,128,128]{2,1,0:T(8,128)} %fusion.84, f32[108,128,128]{2,1,0:T(8,128)} %get-tuple-element.286, f32[108,128,128]{2,1,0:T(8,128)} %fusion.83, f32[3,108,128]{2,1,0:T(8,128)S(1)} %copy.575, f32[3,108,128]{2,1,0:T(8,128)} %sub.460, f32[3,108,128]{2,1,0:T(8,128)S(1)} %copy.572, ...), kind=kLoop, calls=%fused_computation.17.clone.1 | loop fusion | flops 40697856 | bytes 28975104 | tf_op jit(solution)/shard_map/while/body/eval_jaxpr/reduce_sum | solution.py:90
  157.3 10.0 %rsqrt_multiply_fusion.2 = f32[108,128,128]{2,1,0:T(8,128)S(1)} fusion(f32[108,128,128]{2,1,0:T(8,128)} %multiply_reduce_fusion.5, f32[108,128]{1,0:T(8,128)S(1)} %bitcast.424, f32[108,128]{1,0:T(8,128)S(1)} %broadcast_in_dim.173, f32[108,128,128]{2,1,0:T(8,128)} %fusion.82), kind=kLoop, calls=%fused_computation.26.clone.1 | loop fusion | flops 24772608 | bytes 21344256 | tf_op jit(solution)/shard_map/while/body/eval_jaxpr/div | solution.py:89
  172.9 21.9 %multiply_reduce_fusion.6 = f32[3,108,128]{2,1,0:T(8,128)S(1)} fusion(f32[108,128,128]{2,1,0:T(8,128)} %multiply_subtract_fusion.8, f32[108,128,128]{2,1,0:T(8,128)S(1)} %rsqrt_multiply_fusion.2, f32[108,128,128]{2,1,0:T(8,128)} %fusion.84, f32[108,128,128]{2,1,0:T(8,128)S(1)} %copy-done, f32[108,128,128]{2,1,0:T(8,128)} %get-tuple-element.287, ...), kind=kLoop, calls=%fused_computation.16.clone.1 | loop fusion | flops 58351104 | bytes 43296768 | tf_op jit(solution)/shard_map/while/body/eval_jaxpr/reduce_sum | solution.py:93
  198.1 9.8 %fusion.82 = f32[108,128,128]{2,1,0:T(8,128)} fusion(f32[3,108,128]{2,1,0:T(8,128)S(1)} %copy.572, f32[3,108,128]{2,1,0:T(8,128)S(1)} %sub.459), kind=kLoop, calls=%fused_computation.13.clone.1 | loop fusion | flops 14155776 | bytes 7409664 | tf_op jit(solution)/shard_map/while/body/eval_jaxpr/reduce_sum | solution.py:75
  208.0 7.6 %fusion.83 = f32[108,128,128]{2,1,0:T(8,128)} fusion(f32[108,128,128]{2,1,0:T(8,128)} %fusion.82, f32[108,128]{1,0:T(8,128)S(1)} %bitcast.422, f32[108,128]{1,0:T(8,128)S(1)} %broadcast_in_dim.173), kind=kLoop, calls=%fused_computation.23.clone.4 | loop fusion | flops 5308416 | bytes 14266368 | tf_op jit(solution)/shard_map/while/body/eval_jaxpr/max | solution.py:76
  218.1 18.8 %fusion.84 = f32[108,128,128]{2,1,0:T(8,128)} fusion(f32[108,128,128]{2,1,0:T(8,128)} %fusion.83, f32[3,108,128]{2,1,0:T(8,128)S(1)} %copy.575, f32[3,108,128]{2,1,0:T(8,128)} %sub.460, f32[3,108,128]{2,1,0:T(8,128)S(1)} %copy.572, f32[3,108,128]{2,1,0:T(8,128)S(1)} %sub.459), kind=kLoop, calls=%fused_computation.14.clone.1 | loop fusion | flops 24772608 | bytes 14819328 | tf_op jit(solution)/shard_map/while/body/eval_jaxpr/reduce_sum | solution.py:82
  236.9 11.4 %add_multiply_fusion.9 = (f32[108,128,128]{2,1,0:T(8,128)}, f32[108,128,128]{2,1,0:T(8,128)}) fusion(f32[108,128,128]{2,1,0:T(8,128)} %fusion.84, f32[108,128]{1,0:T(8,128)S(1)} %bitcast.423, f32[108,128]{1,0:T(8,128)S(1)} %broadcast_in_dim.173, f32[108,128,128]{2,1,0:T(8,128)S(1)} %bitcast.418), kind=kLoop, calls=%fused_computation.27.clone.1 | loop fusion | flops 24772608 | bytes 28422144 | tf_op jit(solution)/shard_map/while/body/eval_jaxpr/mul | solution.py:84
  248.2 19.0 %multiply_reduce_fusion.5 = f32[108,128,128]{2,1,0:T(8,128)} fusion(f32[108,128,128]{2,1,0:T(8,128)} %fusion.84, f32[108,128,128]{2,1,0:T(8,128)} %get-tuple-element.286, f32[108,128,128]{2,1,0:T(8,128)} %fusion.83, f32[3,108,128]{2,1,0:T(8,128)S(1)} %copy.575, f32[3,108,128]{2,1,0:T(8,128)} %sub.460, f32[3,108,128]{2,1,0:T(8,128)S(1)} %copy.572, ...), kind=kLoop, calls=%fused_computation.17.clone.1 | loop fusion | flops 40697856 | bytes 28975104 | tf_op jit(solution)/shard_map/while/body/eval_jaxpr/reduce_sum | solution.py:90
  267.3 10.0 %rsqrt_multiply_fusion.2 = f32[108,128,128]{2,1,0:T(8,128)S(1)} fusion(f32[108,128,128]{2,1,0:T(8,128)} %multiply_reduce_fusion.5, f32[108,128]{1,0:T(8,128)S(1)} %bitcast.424, f32[108,128]{1,0:T(8,128)S(1)} %broadcast_in_dim.173, f32[108,128,128]{2,1,0:T(8,128)} %fusion.82), kind=kLoop, calls=%fused_computation.26.clone.1 | loop fusion | flops 24772608 | bytes 21344256 | tf_op jit(solution)/shard_map/while/body/eval_jaxpr/div | solution.py:89
  282.9 21.9 %multiply_reduce_fusion.6 = f32[3,108,128]{2,1,0:T(8,128)S(1)} fusion(f32[108,128,128]{2,1,0:T(8,128)} %multiply_subtract_fusion.8, f32[108,128,128]{2,1,0:T(8,128)S(1)} %rsqrt_multiply_fusion.2, f32[108,128,128]{2,1,0:T(8,128)} %fusion.84, f32[108,128,128]{2,1,0:T(8,128)S(1)} %copy-done, f32[108,128,128]{2,1,0:T(8,128)} %get-tuple-element.287, ...), kind=kLoop, calls=%fused_computation.16.clone.1 | loop fusion | flops 58351104 | bytes 43296768 | tf_op jit(solution)/shard_map/while/body/eval_jaxpr/reduce_sum | solution.py:93
  308.1 9.8 %fusion.82 = f32[108,128,128]{2,1,0:T(8,128)} fusion(f32[3,108,128]{2,1,0:T(8,128)S(1)} %copy.572, f32[3,108,128]{2,1,0:T(8,128)S(1)} %sub.459), kind=kLoop, calls=%fused_computation.13.clone.1 | loop fusion | flops 14155776 | bytes 7409664 | tf_op jit(solution)/shard_map/while/body/eval_jaxpr/reduce_sum | solution.py:75
  318.0 7.6 %fusion.83 = f32[108,128,128]{2,1,0:T(8,128)} fusion(f32[108,128,128]{2,1,0:T(8,128)} %fusion.82, f32[108,128]{1,0:T(8,128)S(1)} %bitcast.422, f32[108,128]{1,0:T(8,128)S(1)} %broadcast_in_dim.173), kind=kLoop, calls=%fused_computation.23.clone.4 | loop fusion | flops 5308416 | bytes 14266368 | tf_op jit(solution)/shard_map/while/body/eval_jaxpr/max | solution.py:76
  328.1 18.8 %fusion.84 = f32[108,128,128]{2,1,0:T(8,128)} fusion(f32[108,128,128]{2,1,0:T(8,128)} %fusion.83, f32[3,108,128]{2,1,0:T(8,128)S(1)} %copy.575, f32[3,108,128]{2,1,0:T(8,128)} %sub.460, f32[3,108,128]{2,1,0:T(8,128)S(1)} %copy.572, f32[3,108,128]{2,1,0:T(8,128)S(1)} %sub.459), kind=kLoop, calls=%fused_computation.14.clone.1 | loop fusion | flops 24772608 | bytes 14819328 | tf_op jit(solution)/shard_map/while/body/eval_jaxpr/reduce_sum | solution.py:82
  346.9 11.4 %add_multiply_fusion.9 = (f32[108,128,128]{2,1,0:T(8,128)}, f32[108,128,128]{2,1,0:T(8,128)}) fusion(f32[108,128,128]{2,1,0:T(8,128)} %fusion.84, f32[108,128]{1,0:T(8,128)S(1)} %bitcast.423, f32[108,128]{1,0:T(8,128)S(1)} %broadcast_in_dim.173, f32[108,128,128]{2,1,0:T(8,128)S(1)} %bitcast.418), kind=kLoop, calls=%fused_computation.27.clone.1 | loop fusion | flops 24772608 | bytes 28422144 | tf_op jit(solution)/shard_map/while/body/eval_jaxpr/mul | solution.py:84
  358.2 19.0 %multiply_reduce_fusion.5 = f32[108,128,128]{2,1,0:T(8,128)} fusion(f32[108,128,128]{2,1,0:T(8,128)} %fusion.84, f32[108,128,128]{2,1,0:T(8,128)} %get-tuple-element.286, f32[108,128,128]{2,1,0:T(8,128)} %fusion.83, f32[3,108,128]{2,1,0:T(8,128)S(1)} %copy.575, f32[3,108,128]{2,1,0:T(8,128)} %sub.460, f32[3,108,128]{2,1,0:T(8,128)S(1)} %copy.572, ...), kind=kLoop, calls=%fused_computation.17.clone.1 | loop fusion | flops 40697856 | bytes 28975104 | tf_op jit(solution)/shard_map/while/body/eval_jaxpr/reduce_sum | solution.py:90
  377.3 10.0 %rsqrt_multiply_fusion.2 = f32[108,128,128]{2,1,0:T(8,128)S(1)} fusion(f32[108,128,128]{2,1,0:T(8,128)} %multiply_reduce_fusion.5, f32[108,128]{1,0:T(8,128)S(1)} %bitcast.424, f32[108,128]{1,0:T(8,128)S(1)} %broadcast_in_dim.173, f32[108,128,128]{2,1,0:T(8,128)} %fusion.82), kind=kLoop, calls=%fused_computation.26.clone.1 | loop fusion | flops 24772608 | bytes 21344256 | tf_op jit(solution)/shard_map/while/body/eval_jaxpr/div | solution.py:89
  392.9 21.9 %multiply_reduce_fusion.6 = f32[3,108,128]{2,1,0:T(8,128)S(1)} fusion(f32[108,128,128]{2,1,0:T(8,128)} %multiply_subtract_fusion.8, f32[108,128,128]{2,1,0:T(8,128)S(1)} %rsqrt_multiply_fusion.2, f32[108,128,128]{2,1,0:T(8,128)} %fusion.84, f32[108,128,128]{2,1,0:T(8,128)S(1)} %copy-done, f32[108,128,128]{2,1,0:T(8,128)} %get-tuple-element.287, ...), kind=kLoop, calls=%fused_computation.16.clone.1 | loop fusion | flops 58351104 | bytes 43296768 | tf_op jit(solution)/shard_map/while/body/eval_jaxpr/reduce_sum | solution.py:93
  418.1 9.8 %fusion.82 = f32[108,128,128]{2,1,0:T(8,128)} fusion(f32[3,108,128]{2,1,0:T(8,128)S(1)} %copy.572, f32[3,108,128]{2,1,0:T(8,128)S(1)} %sub.459), kind=kLoop, calls=%fused_computation.13.clone.1 | loop fusion | flops 14155776 | bytes 7409664 | tf_op jit(solution)/shard_map/while/body/eval_jaxpr/reduce_sum | solution.py:75
  438.1 18.8 %fusion.84 = f32[108,128,128]{2,1,0:T(8,128)} fusion(f32[108,128,128]{2,1,0:T(8,128)} %fusion.83, f32[3,108,128]{2,1,0:T(8,128)S(1)} %copy.575, f32[3,108,128]{2,1,0:T(8,128)} %sub.460, f32[3,108,128]{2,1,0:T(8,128)S(1)} %copy.572, f32[3,108,128]{2,1,0:T(8,128)S(1)} %sub.459), kind=kLoop, calls=%fused_computation.14.clone.1 | loop fusion | flops 24772608 | bytes 14819328 | tf_op jit(solution)/shard_map/while/body/eval_jaxpr/reduce_sum | solution.py:82
  456.9 11.4 %add_multiply_fusion.9 = (f32[108,128,128]{2,1,0:T(8,128)}, f32[108,128,128]{2,1,0:T(8,128)}) fusion(f32[108,128,128]{2,1,0:T(8,128)} %fusion.84, f32[108,128]{1,0:T(8,128)S(1)} %bitcast.423, f32[108,128]{1,0:T(8,128)S(1)} %broadcast_in_dim.173, f32[108,128,128]{2,1,0:T(8,128)S(1)} %bitcast.418), kind=kLoop, calls=%fused_computation.27.clone.1 | loop fusion | flops 24772608 | bytes 28422144 | tf_op jit(solution)/shard_map/while/body/eval_jaxpr/mul | solution.py:84
  468.2 19.0 %multiply_reduce_fusion.5 = f32[108,128,128]{2,1,0:T(8,128)} fusion(f32[108,128,128]{2,1,0:T(8,128)} %fusion.84, f32[108,128,128]{2,1,0:T(8,128)} %get-tuple-element.286, f32[108,128,128]{2,1,0:T(8,128)} %fusion.83, f32[3,108,128]{2,1,0:T(8,128)S(1)} %copy.575, f32[3,108,128]{2,1,0:T(8,128)} %sub.460, f32[3,108,128]{2,1,0:T(8,128)S(1)} %copy.572, ...), kind=kLoop, calls=%fused_computation.17.clone.1 | loop fusion | flops 40697856 | bytes 28975104 | tf_op jit(solution)/shard_map/while/body/eval_jaxpr/reduce_sum | solution.py:90
  487.3 10.0 %rsqrt_multiply_fusion.2 = f32[108,128,128]{2,1,0:T(8,128)S(1)} fusion(f32[108,128,128]{2,1,0:T(8,128)} %multiply_reduce_fusion.5, f32[108,128]{1,0:T(8,128)S(1)} %bitcast.424, f32[108,128]{1,0:T(8,128)S(1)} %broadcast_in_dim.173, f32[108,128,128]{2,1,0:T(8,128)} %fusion.82), kind=kLoop, calls=%fused_computation.26.clone.1 | loop fusion | flops 24772608 | bytes 21344256 | tf_op jit(solution)/shard_map/while/body/eval_jaxpr/div | solution.py:89
  502.9 21.9 %multiply_reduce_fusion.6 = f32[3,108,128]{2,1,0:T(8,128)S(1)} fusion(f32[108,128,128]{2,1,0:T(8,128)} %multiply_subtract_fusion.8, f32[108,128,128]{2,1,0:T(8,128)S(1)} %rsqrt_multiply_fusion.2, f32[108,128,128]{2,1,0:T(8,128)} %fusion.84, f32[108,128,128]{2,1,0:T(8,128)S(1)} %copy-done, f32[108,128,128]{2,1,0:T(8,128)} %get-tuple-element.287, ...), kind=kLoop, calls=%fused_computation.16.clone.1 | loop fusion | flops 58351104 | bytes 43296768 | tf_op jit(solution)/shard_map/while/body/eval_jaxpr/reduce_sum | solution.py:93
  528.8 12.6 %scatter_custom_fusion.1 = f32[512,6]{1,0:T(8,128)S(1)} fusion(s32[2048]{0:T(1024)S(1)} %bitcast.457, f32[2048,6]{1,0:T(8,128)S(1)} %copy.516, f32[]{:T(128)} %constant.324.clone.1), kind=kCustom, calls=%fused_computation.87 | custom fusion | flops 12288 | bytes 12292 | tf_op jit(solution)/shard_map/scatter-add | solution.py:292
  541.4 24.7 %scatter_fusion.1 = f32[9,128,6]{2,1,0:T(8,128)S(1)} fusion(f32[9,128,6]{2,1,0:T(8,128)S(1)} %broadcast_in_dim.124, s32[512]{0:T(512)} %bitcast.420, f32[512,6]{1,0:T(8,128)S(1)} %scatter_custom_fusion.1), kind=kCustom, calls=%fused_computation.7 | custom fusion | bytes 40960 | tf_op jit(solution)/shard_map/scatter | solution.py:301
  587.2 9.6 %scatter_custom_fusion.3 = f32[257,6]{1,0:T(8,128)S(1)} fusion(s32[1152]{0:T(1024)S(1)} %reshape.1086, f32[1152,6]{1,0:T(8,128)S(1)} %copy.522, f32[]{:T(128)} %constant.324.clone.1), kind=kCustom, calls=%fused_computation.91 | custom fusion | flops 6912 | bytes 6172 | tf_op jit(solution)/shard_map/scatter-add | solution.py:331
  (432 shorter events, 146.9 us)
Async XLA Ops:
  1.4 72.1 %collective-permute-start.4 = (f32[7,1,2,8,128]{4,3,2,1,0:T(8,128)S(1)}, f32[7,1,2,8,128]{4,3,2,1,0:T(8,128)S(1)}, u32[]{:S(2)}, u32[]{:S(2)}) collective-permute-start(f32[7,1,2,8,128]{4,3,2,1,0:T(8,128)S(1)} %pad_maximum_fusion.5), channel_id=1, source_target_pairs={{0,8},{8,16},{16,24},{24,32},{32,40},{40,48},{48,56},{56,64},{64,7... | collective-permute-start | bytes 172040 | tf_op jit(solution)/shard_map/ppermute | solution.py:30
  3.9 69.6 %collective-permute-start.5 = (f32[7,1,2,8,128]{4,3,2,1,0:T(8,128)S(1)}, f32[7,1,2,8,128]{4,3,2,1,0:T(8,128)S(1)}, u32[]{:S(2)}, u32[]{:S(2)}) collective-permute-start(f32[7,1,2,8,128]{4,3,2,1,0:T(8,128)S(1)} %pad_maximum_fusion.5), channel_id=1, source_target_pairs={{8,0},{16,8},{24,16},{32,24},{40,32},{48,40},{56,48},{64,56},{72,6... | collective-permute-start | bytes 172040 | tf_op jit(solution)/shard_map/ppermute | solution.py:31
  12.7 72.7 %copy-start.1 = (s32[512,1]{0,1:T(1,128)}, s32[512,1]{0,1:T(1,128)S(1)}, u32[]{:S(2)}) copy-start(s32[512,1]{0,1:T(1,128)S(1)} %get-tuple-element.163) | copy-start | bytes 6148
  55.8 9.8 %collective-permute-start = (s32[3,128]{1,0:T(4,128)S(1)}, s32[3,128]{1,0:T(4,128)S(1)}, u32[]{:S(2)}, u32[]{:S(2)}) collective-permute-start(s32[3,128]{1,0:T(4,128)S(1)} %get-tuple-element.200), channel_id=1, source_target_pairs={{0,120},{8,0},{16,8},{24,16},{32,24},{40,32},{48,40},{56,48},{64,5... | collective-permute-start | bytes 4616 | tf_op jit(solution)/shard_map/ppermute | solution.py:39
  57.3 8.4 %collective-permute-start.1 = (s32[3,128]{1,0:T(4,128)S(1)}, s32[3,128]{1,0:T(4,128)S(1)}, u32[]{:S(2)}, u32[]{:S(2)}) collective-permute-start(s32[3,128]{1,0:T(4,128)S(1)} %get-tuple-element.201), channel_id=1, source_target_pairs={{0,8},{8,16},{16,24},{24,32},{32,40},{40,48},{48,56},{56,64},{64,7... | collective-permute-start | bytes 4616 | tf_op jit(solution)/shard_map/ppermute | solution.py:39
  65.7 7.0 %collective-permute-start.2 = (s32[3,128]{1,0:T(4,128)S(1)}, s32[3,128]{1,0:T(4,128)S(1)}, u32[]{:S(2)}, u32[]{:S(2)}) collective-permute-start(s32[3,128]{1,0:T(4,128)S(1)} %bitcast.486), channel_id=1, source_target_pairs={{1,0},{2,1},{3,2},{4,3},{5,4},{6,5},{7,6},{9,8},{10,9},{11,10},{12... | collective-permute-start | bytes 4616 | tf_op jit(solution)/shard_map/ppermute | solution.py:45
  69.1 3.8 collective-permute-start.3
  74.3 6.9 %collective-permute-start.6 = (f32[7,3,1,8,128]{4,3,2,1,0:T(8,128)S(1)}, f32[7,3,1,8,128]{4,3,2,1,0:T(8,128)S(1)}, u32[]{:S(2)}, u32[]{:S(2)}) collective-permute-start(f32[7,3,1,8,128]{4,3,2,1,0:T(8,128)S(1)} %get-tuple-element.183), channel_id=1, source_target_pairs={{0,1},{1,2},{2,3},{3,4},{4,5},{5,6},{6,7},{8,9},{9,10},{10,11},{11... | collective-permute-start | bytes 258056 | tf_op jit(solution)/shard_map/ppermute | solution.py:30
  78.5 5.8 collective-permute-start.7
  85.3 441.0 %copy-start.8 = (f32[1,2,8,128]{3,2,1,0:T(8,128)S(1)}, f32[1,2,8,128]{3,2,1,0:T(8,128)}, u32[]{:S(2)}) copy-start(f32[1,2,8,128]{3,2,1,0:T(8,128)} %get-tuple-element.161) | copy-start | bytes 24580
  85.3 441.0 %copy-start.13 = (f32[1,1,2,8,128]{4,3,2,0,1:T(8,128)S(1)}, f32[1,1,2,8,128]{4,3,2,0,1:T(8,128)}, u32[]{:S(2)}) copy-start(f32[1,1,2,8,128]{4,3,2,0,1:T(8,128)} %fusion.60) | copy-start | bytes 24580
  85.4 442.3 %copy-start.9 = (f32[1,2,8,128]{3,2,1,0:T(8,128)S(1)}, f32[1,2,8,128]{3,2,1,0:T(8,128)}, u32[]{:S(2)}) copy-start(f32[1,2,8,128]{3,2,1,0:T(8,128)} %broadcast_multiply_fusion.1) | copy-start | bytes 24580
  85.4 443.4 %copy-start.10 = (s32[1,1,2048]{2,1,0:T(1,128)S(1)}, s32[1,1,2048]{2,1,0:T(1,128)}, u32[]{:S(2)}) copy-start(s32[1,1,2048]{2,1,0:T(1,128)} %param.20) | copy-start | bytes 24580
  525.4 45.9 %copy-start.17 = (s32[3,128]{1,0:T(4,128)S(1)}, s32[3,128]{1,0:T(4,128)}, u32[]{:S(2)}) copy-start(s32[3,128]{1,0:T(4,128)} %copy-done.16) | copy-start | bytes 4612
  525.4 71.5 %copy-start.22 = (f32[3,1,1,256]{3,2,1,0:T(1,128)S(1)}, f32[3,1,1,256]{3,2,1,0:T(1,128)}, u32[]{:S(2)}) copy-start(f32[3,1,1,256]{3,2,1,0:T(1,128)} %param.26) | copy-start | bytes 9220
  525.4 71.5 %copy-start.24 = (f32[3,1,1,256]{3,2,1,0:T(1,128)S(1)}, f32[3,1,1,256]{3,2,1,0:T(1,128)}, u32[]{:S(2)}) copy-start(f32[3,1,1,256]{3,2,1,0:T(1,128)} %param.28) | copy-start | bytes 9220
  525.4 71.8 %copy-start.20 = (f32[3,1,1,256]{3,2,1,0:T(1,128)S(1)}, f32[3,1,1,256]{3,2,1,0:T(1,128)}, u32[]{:S(2)}) copy-start(f32[3,1,1,256]{3,2,1,0:T(1,128)} %get-tuple-element.205) | copy-start | bytes 9220
  525.5 71.8 %copy-start.21 = (f32[3,1,1,256]{3,2,1,0:T(1,128)S(1)}, f32[3,1,1,256]{3,2,1,0:T(1,128)}, u32[]{:S(2)}) copy-start(f32[3,1,1,256]{3,2,1,0:T(1,128)} %get-tuple-element.206) | copy-start | bytes 9220
  525.5 71.8 %copy-start.23 = (f32[3,1,1,256]{3,2,1,0:T(1,128)S(1)}, f32[3,1,1,256]{3,2,1,0:T(1,128)}, u32[]{:S(2)}) copy-start(f32[3,1,1,256]{3,2,1,0:T(1,128)} %param.24) | copy-start | bytes 9220
  525.5 71.8 %copy-start.25 = (f32[1,1,256]{2,1,0:T(1,128)S(1)}, f32[1,1,256]{2,1,0:T(1,128)}, u32[]{:S(2)}) copy-start(f32[1,1,256]{2,1,0:T(1,128)} %param.27) | copy-start | bytes 3076
  525.5 71.8 %copy-start.26 = (f32[3]{0:T(128)S(1)}, f32[3]{0:T(128)}, u32[]{:S(2)}) copy-start(f32[3]{0:T(128)} %constant.351.clone) | copy-start | bytes 40
  525.5 72.1 %copy-start.15 = (s32[2048]{0:T(1024)S(1)}, s32[2048]{0:T(1024)}, u32[]{:S(2)}) copy-start(s32[2048]{0:T(1024)} %pad_clamp_fusion.2) | copy-start | bytes 24580
  541.4 74.6 %copy-start.3 = (s32[512,1]{0,1:T(1,128)S(1)}, s32[512,1]{0,1:T(1,128)}, u32[]{:S(2)}) copy-start(s32[512,1]{0,1:T(1,128)} %get-tuple-element.164) | copy-start | bytes 6148
  566.1 53.6 %copy-start.14 = (s32[2048]{0:T(1024)S(1)}, s32[2048]{0:T(1024)}, u32[]{:S(2)}) copy-start(s32[2048]{0:T(1024)} %broadcast_clamp_fusion) | copy-start | bytes 24580
  566.2 7.8 %collective-permute-start.8 = (f32[3,128,6]{2,1,0:T(8,128)S(1)}, f32[3,128,6]{2,1,0:T(8,128)S(1)}, u32[]{:S(2)}, u32[]{:S(2)}) collective-permute-start(f32[3,128,6]{2,1,0:T(8,128)S(1)} %get-tuple-element.180), channel_id=1, source_target_pairs={{0,120},{8,0},{16,8},{24,16},{32,24},{40,32},{48,40},{56,48},{64,5... | collective-permute-start | bytes 27656 | tf_op jit(solution)/shard_map/ppermute | solution.py:39
  571.3 8.2 %collective-permute-start.9 = (f32[3,128,6]{2,1,0:T(8,128)S(1)}, f32[3,128,6]{2,1,0:T(8,128)S(1)}, u32[]{:S(2)}, u32[]{:S(2)}) collective-permute-start(f32[3,128,6]{2,1,0:T(8,128)S(1)} %get-tuple-element.181), channel_id=1, source_target_pairs={{0,8},{8,16},{16,24},{24,32},{32,40},{40,48},{48,56},{56,64},{64,7... | collective-permute-start | bytes 27656 | tf_op jit(solution)/shard_map/ppermute | solution.py:39
  579.6 6.6 %collective-permute-start.10 = (f32[3,128,6]{1,2,0:T(8,128)S(1)}, f32[3,128,6]{1,2,0:T(8,128)S(1)}, u32[]{:S(2)}, u32[]{:S(2)}) collective-permute-start(f32[3,128,6]{1,2,0:T(8,128)S(1)} %get-tuple-element.194), channel_id=1, source_target_pairs={{1,0},{2,1},{3,2},{4,3},{5,4},{6,5},{7,6},{9,8},{10,9},{11,10},{12... | collective-permute-start | bytes 27656 | tf_op jit(solution)/shard_map/ppermute | solution.py:45
  581.5 5.4 collective-permute-start.11
  600.3 6.2 collective-permute-start.12
  604.6 5.1 collective-permute-start.13
  609.7 6.1 collective-permute-start.14
  609.8 6.0 collective-permute-start.15
  (37 other events, 682.7 us)
where the time goes:
time: 629 us; the launch traced here: 626 us
  other arithmetic  450 us (72%)
  local copies, waits for them, and re-layouts  113 us (18%)
  starting transfers between devices  44 us (7%)
  waiting for transfers between devices  15.8 us (3%)
    reduce_sum x4, other arithmetic, pair_force(): return jnp.sum(forces, 3)  87.4 us
    reduce_sum x4, other arithmetic, pair_force(): jnp.sum(shear_force * shear_force, 0) + friction_cap * friction_cap + 1e-06  76.1 us
    reduce_sum x4, other arithmetic, pair_force(): normal_speed = jnp.sum(relative * normal, 0)  75.1 us
    mul x4, other arithmetic, pair_force(): stiff_root * (STIFFNESS * intersection - NORMAL_DAMPING * normal_speed -...  45.5 us
    scatter x1, local copies, waits for them, and re-layouts, on_device(): jnp.full((9, capacity), clump_count, jnp.int32).at[codes, slots]  43.1 us
    div x4, other arithmetic, pair_force(): friction_cap / jnp.sqrt(jnp.sum(shear_force * shear_force, 0) + friction_...  40.1 us
    reduce_sum x4, other arithmetic, pair_force(): distance = jnp.sqrt(jnp.sum(separation * separation, 0))  39.1 us
    max x4, other arithmetic, pair_force(): distance = jnp.maximum(distance, 0.25 * radius_sum)  30.6 us
  transfers between devices with their start and end apart: 16, of which 7 were waited for; matrix products, arithmetic and copies ran while one was open for 9% of the time, Pallas kernels for 0%

commit v1 on v0

v1 whole, which is shorter than its diff:
```python
import functools
import math

import jax
import jax.numpy as jnp
from jax import lax
from jax.experimental import pallas as pl
from jax.experimental.pallas import tpu as pltpu
from jax.sharding import PartitionSpec as P

PHASES = 64
CELL_SIDE = 5.0
BLADE_STIFFNESS = 20.0
BLADE_THICKNESS = 1.0
TIME_STEP = 0.5
GRAVITY = 0.5

REACH = 1.2001
CHUNK = 32
F32 = jnp.float32
BF16 = jnp.bfloat16
MESH = pl.DeviceIdType.MESH
LANES = (((1,), (1,)), ((), ()))
ROWS = (((1,), (0,)), ((), ()))
VMEM = pl.BlockSpec(memory_space=pltpu.VMEM)
SMEM = pl.BlockSpec(memory_space=pltpu.SMEM)
ANY = pl.BlockSpec(memory_space=pl.ANY)


def split3(x):
    high = x.astype(BF16)
    rest = x - high.astype(F32)
    middle = rest.astype(BF16)
    low = (rest - middle.astype(F32)).astype(BF16)
    return high, middle, low


def rows3(x):
    high = x.astype(BF16).astype(F32)
    rest = x - high
    middle = rest.astype(BF16).astype(F32)
    return jnp.concatenate([high, middle, rest - middle], 0).astype(BF16)


def sum3(x):
    return x[0:8] + x[8:16] + x[16:24]


def one_hot(rows, row):
    length = row.shape[-1]
    ids = lax.broadcasted_iota(jnp.int32, (rows, length), 0)
    return jnp.where(ids == row, 1.0, 0.0).astype(BF16)


class Place:
    def __init__(self, n_shaft, n_lat):
        self.n_shaft, self.n_lat = n_shaft, n_lat
        self.s, self.l = lax.axis_index("shaft"), lax.axis_index("lat")

    def at(self, ds, dl):
        return {"shaft": lax.rem(self.s + ds + self.n_shaft, self.n_shaft), "lat": self.l + dl}

    def lateral(self, act):
        act(0)
        pl.when(self.l > 0)(lambda: act(-1))
        pl.when(self.l < self.n_lat - 1)(lambda: act(1))

    def barrier(self):
        sem = pltpu.get_barrier_semaphore()

        def signal(dl):
            for ds in (-1, 0, 1):
                if (ds, dl) != (0, 0):
                    pl.semaphore_signal(
                        sem, inc=1, device_id=self.at(ds, dl), device_id_type=MESH
                    )

        self.lateral(signal)
        edge = jnp.logical_or(self.l == 0, self.l == self.n_lat - 1)
        pl.semaphore_wait(sem, jnp.where(edge, 5, 8))


def halo_kernel(n_shaft, n_lat, pos, vel, rad, ext, send_sem, recv_sem, own_sem):
    place = Place(n_shaft, n_lat)

    def parts(j, si, lj):
        return (
            (pos.at[:, 0, j], ext.at[si, lj, 0:3]),
            (vel.at[:, 0, j], ext.at[si, lj, 3:6]),
            (rad.at[0, pl.ds(j, 1)], ext.at[si, lj, 6:7]),
        )

    def remote(j, ds, dl, si, lj):
        return [
            pltpu.make_async_remote_copy(
                src_ref=src,
                dst_ref=dst,
                send_sem=send_sem.at[si, lj, t],
                recv_sem=recv_sem.at[si, lj, t],
                device_id=place.at(ds, dl),
                device_id_type=MESH,
            )
            for t, (src, dst) in enumerate(parts(j, si, lj))
        ]

    def outgoing(dl):
        found = []
        for ds in (-1, 0, 1):
            for j in (0, 1):
                lj = j - 2 * dl + 1
                if 0 <= lj <= 3 and (ds, dl) != (0, 0):
                    found += remote(j, ds, dl, 1 - ds, lj)
        return found

    def incoming(dl):
        found = []
        for ds in (-1, 0, 1):
            for lj in {0: (1, 2), -1: (0,), 1: (3,)}[dl]:
                if (ds, dl) != (0, 0):
                    found += remote(0, ds, dl, 1 + ds, lj)
        return found

    own = [
        pltpu.make_async_copy(src, dst, own_sem.at[j, t])
        for j in (0, 1)
        for t, (src, dst) in enumerate(parts(j, 1, 1 + j))
    ]
    place.barrier()
    place.lateral(lambda dl: [c.start() for c in outgoing(dl)] and None)
    for c in own:
        c.start()
    ext[:, :, 7] = jnp.zeros((3, 4, 8, 128), F32)

    @pl.when(place.l == 0)
    def _():
        ext[:, 0, 0:7] = jnp.zeros((3, 7, 8, 128), F32)

    @pl.when(place.l == n_lat - 1)
    def _():
        ext[:, 3, 0:7] = jnp.zeros((3, 7, 8, 128), F32)

    for c in own:
        c.wait()
    place.lateral(lambda dl: [c.wait_recv() for c in incoming(dl)] and None)
    place.lateral(lambda dl: [c.wait_send() for c in outgoing(dl)] and None)


def pair_sums(mine, other, acc):
    ax, ay, az, au, av, aw, ar, ar4 = mine
    bx, by, bz, bu, bv, bw, br = other
    dx, dy, dz = ax - bx, ay - by, az - bz
    square = dx * dx + dy * dy + dz * dz
    radii = ar + br
    clamped = jnp.maximum(square, radii * radii * 0.0625)
    inverse = lax.rsqrt(clamped)
    delta = jnp.maximum(radii - clamped * inverse, 0.0)
    du, dv, dw = au - bu, av - bv, aw - bw
    normal_speed = (du * dx + dv * dy + dw * dz) * inverse
    speed = du * du + dv * dv + dw * dw
    unit = square * (inverse * inverse)
    sliding = jnp.maximum(speed + normal_speed * normal_speed * (unit - 2.0), 0.0)
    load = ar4 * br * delta
    root = load * lax.rsqrt(jnp.maximum(load * radii, 1e-30))
    root2 = root * root
    cap = 2.5 * delta
    shear = root2 * cap * lax.rsqrt(root2 * (sliding + cap * cap) + 1e-06)
    push = root * (5.0 * delta - normal_speed - 0.25)
    along = (push + shear * normal_speed) * inverse
    return (
        acc[0] + (along * dx - shear * du),
        acc[1] + (along * dy - shear * dv),
        acc[2] + (along * dz - shear * dw),
    )


def contact_kernel(
    lat_cells,
    phase,
    ext,
    off,
    piece,
    route,
    clump,
    angles,
    inertia,
    part,
    turning,
    dest,
    count_v,
    count_s,
    bounds,
    picked,
    packed,
    force,
    copy_sem,
):
    sub = lax.broadcasted_iota(jnp.int32, (8, 128), 0)

    before = jnp.where(
        lax.broadcasted_iota(jnp.int32, (128, 128), 0)
        < lax.broadcasted_iota(jnp.int32, (128, 128), 1),
        1.0,
        0.0,
    ).astype(BF16)
    ones = jnp.ones((128, 128), BF16)
    for j in range(2):
        masks = []
        for c in range(9):
            di, dj = c // 3 - 1, c % 3 - 1
            base = ((1 + di) * 4 + 1 + j + dj) * 64
            x, y, z = (ext[base + 8 * t : base + 8 * t + 8, :] for t in range(3))
            keep = ext[base + 48 : base + 56, :] > 0.0
            if di:
                keep &= (x < REACH) if di > 0 else (x > CELL_SIDE - REACH)
            if dj:
                keep &= (y < REACH) if dj > 0 else (y > CELL_SIDE - REACH)
            low, high = z < REACH, z > CELL_SIDE - REACH
            kept = jnp.where(keep, 1.0, 0.0)
            low_f = jnp.where(low, kept, 0.0)
            high_f = jnp.where(high, kept, 0.0)
            masks += [low_f, kept - low_f - high_f, high_f]
        mask_f = jnp.concatenate(masks, 0)
        mask = mask_f.astype(BF16)
        prefix = lax.dot_general(mask, before, ROWS, preferred_element_type=F32)
        total = lax.dot_general(mask, ones, ROWS, preferred_element_type=F32)
        counts = lax.dot_general(ones[0:8], mask, LANES, preferred_element_type=F32)
        count_v[:, j * 256 : j * 256 + 216] = counts.astype(jnp.int32)
        for c in range(9):
            a = c * 24
            low_p, mid_p, high_p = (prefix[a + 8 * t : a + 8 * t + 8] for t in range(3))
            low_n, mid_n = total[a : a + 8], total[a + 8 : a + 16]
            spot = (
                masks[3 * c] * low_p
                + masks[3 * c + 1] * (low_n + mid_p)
                + masks[3 * c + 2] * (low_n + mid_n + high_p)
            )
            any_of = masks[3 * c] + masks[3 * c + 1] + masks[3 * c + 2]
            spot = jnp.where(any_of > 0.0, spot, -1.0).astype(jnp.int32)
            dest[(j * 9 + c) * 8 : (j * 9 + c) * 8 + 8, :] = spot
    copy = pltpu.make_async_copy(count_v, count_s, copy_sem)
    copy.start()
    copy.wait()

    for j in range(2):

        def count(c, part_id, k):
            return count_s[0, j * 256 + (c * 3 + part_id) * 8 + k]

        def gather_level(k, offset):
            rise = CELL_SIDE * k.astype(F32) - 20.0
            for c in range(9):
                di, dj = c // 3 - 1, c % 3 - 1
                base = ((1 + di) * 4 + 1 + j + dj) * 64
                value = ext[pl.ds(base + k, 8, stride=8), :]
                shift = jnp.where(
                    sub == 0,
                    CELL_SIDE * di,
                    jnp.where(sub == 1, CELL_SIDE * dj, jnp.where(sub == 2, rise, 0.0)),
                )
                value = jnp.concatenate(split3(value + shift), 1)
                spot = dest[pl.ds((j * 9 + c) * 8 + k, 1), :]

                def pick(first, last):
                    ids = lax.broadcasted_iota(jnp.int32, (last - first, 128), 0) + first
                    hot = jnp.where(ids == spot, 1.0, 0.0).astype(BF16)
                    picked[c, first:last, :] = lax.dot_general(
                        jnp.concatenate([hot, hot, hot], 1),
                        value,
                        LANES,
                        preferred_element_type=F32,
                    )

                if c == 4:
                    pick(0, 128)
                else:
                    pick(0, 64)
                    full = count(c, 0, k) + count(c, 1, k) + count(c, 2, k)
                    pl.when(full > 64)(lambda: pick(64, 128))
            for t in range(3):
                if t == 2:
                    bounds[0, k] = offset
                for c in range(9):
                    amount = count(c, t, k)
                    start = 0 if t == 0 else count(c, 0, k)
                    if t == 2:
                        start = start + count(c, 1, k)
                    short = (64 if t != 1 else 96) if c == 4 else 32

                    def move(first, length):
                        packed[pl.ds(offset + first, length), :] = picked[
                            c, pl.ds(start + first, length), :
                        ]

                    move(0, short)
                    pl.when(amount > short)(lambda: move(short, 128 - short))
                    offset = offset + amount
                if t == 0:
                    bounds[1, k] = offset
            return offset

        end = lax.fori_loop(0, 8, gather_level, jnp.int32(0))
        packed[pl.ds(end, 64), :] = jnp.zeros((64, 8), F32)
        bounds[1, 8] = end

        def cell(k, _):
            rise = CELL_SIDE * k.astype(F32) - 20.0
            base = (5 + j) * 64
            own = [ext[pl.ds(base + 8 * t + k, 1), :] for t in range(7)]
            own[2] = own[2] + rise
            own.append(4.0 * own[6])
            own = [jnp.broadcast_to(v, (8, 128)) for v in own]
            first = jnp.where(k == 0, 0, bounds[0, jnp.maximum(k - 1, 0)])
            first = (first // 8) * 8
            last = bounds[1, k + 1]

            def chunk(i, acc):
                for g in range(CHUNK // 8):
                    at = pl.multiple_of(first + i * CHUNK + g * 8, 8)
                    rows = packed[pl.ds(at, 8), :]
                    acc = pair_sums(own, [rows[:, t : t + 1] for t in range(7)], acc)
                return acc

            zero = jnp.zeros((8, 128), F32)
            sums = lax.fori_loop(
                0, (last - first + CHUNK - 1) // CHUNK, chunk, (zero, zero, zero)
            )
            for t in range(3):
                force[pl.ds((j * 8 + t) * 8 + k, 1), :] = jnp.sum(sums[t], 0, keepdims=True)
            return 0

        lax.fori_loop(0, 8, cell, 0)

    angle = jnp.full((8, 128), phase[0].astype(F32) * (2.0 * math.pi / PHASES), F32)
    cos_b, sin_b = jnp.cos(angle), jnp.sin(angle)
    height_cells = 8
    centre_y, centre_z = 0.5 * CELL_SIDE * lat_cells, 0.5 * CELL_SIDE * height_cells
    reach = 0.45 * CELL_SIDE * min(lat_cells, height_cells)
    shaft_id = lax.axis_index("shaft").astype(F32)
    lat_id = (lax.axis_index("lat") * 2).astype(F32)
    up_id = sub.astype(F32)
    terms = []
    for j in range(2):
        base = (5 + j) * 64
        x, y, z = (ext[base + 8 * t : base + 8 * t + 8, :] for t in range(3))
        radius = ext[base + 48 : base + 56, :]
        x = CELL_SIDE * shaft_id + x
        y = CELL_SIDE * (lat_id + j) + y - centre_y
        z = CELL_SIDE * up_id + z - centre_z
        across = y * cos_b + z * sin_b
        radial = z * cos_b - y * sin_b
        depth = jnp.maximum(jnp.minimum(radius - across, radius + BLADE_THICKNESS + across), 0.0)
        window = jnp.maximum(radial * (reach - radial), 0.0) * (4.0 / (reach * reach))
        gate = jnp.maximum(jnp.cos(x * (2.0 * math.pi / (2.0 * CELL_SIDE))), 0.0)
        size = BLADE_STIFFNESS * depth * window * gate
        fx, fy, fz = (force[(j * 8 + t) * 8 : (j * 8 + t) * 8 + 8, :] for t in range(3))
        fy, fz = fy + size * cos_b, fz + size * sin_b
        ox, oy, oz = (off[t, 0, j] for t in range(3))
        six = [fx, fy, fz, oy * fz - oz * fy, oz * fx - ox * fz, ox * fy - oy * fx]
        for t in range(8):
            force[(j * 8 + t) * 8 : (j * 8 + t) * 8 + 8, :] = (
                six[t] if t < 6 else jnp.zeros((8, 128), F32)
            )
        for k in range(8):
            terms.append(rows3(force[pl.ds(j * 64 + k, 8, stride=8), :]))
    n_piece = route.shape[-1]
    sums = jnp.zeros((24, n_piece), F32)
    for pair in range(8):
        row = piece[0, :, pair * 256 : pair * 256 + 256]
        sums = sums + lax.dot_general(
            jnp.concatenate([terms[2 * pair], terms[2 * pair + 1]], 1),
            one_hot(n_piece, row),
            LANES,
            preferred_element_type=F32,
        )
    sums = rows3(sum3(sums))
    n_clump = part.shape[-1]
    for c in range(9):
        key = jnp.where(route[0] == c, clump[0], -1)
        part[c] = sum3(
            lax.dot_general(sums, one_hot(n_clump, key), LANES, preferred_element_type=F32)
        )

    cos_z, cos_y, cos_x = (jnp.cos(angles[t, 0]) for t in range(3))
    sin_z, sin_y, sin_x = (jnp.sin(angles[t, 0]) for t in range(3))
    rotation = [
        [
            cos_z * cos_y,
            cos_z * sin_y * sin_x - sin_z * cos_x,
            cos_z * sin_y * cos_x + sin_z * sin_x,
        ],
        [
            sin_z * cos_y,
            sin_z * sin_y * sin_x + cos_z * cos_x,
            sin_z * sin_y * cos_x - cos_z * sin_x,
        ],
        [-sin_y, cos_y * sin_x, cos_y * cos_x],
    ]
    for t, (a, b) in enumerate(((0, 0), (0, 1), (0, 2), (1, 1), (1, 2), (2, 2))):
        turning[t : t + 1, :] = TIME_STEP * sum(
            rotation[a][i] * inertia[i, 0] * rotation[b][i] for i in range(3)
        )
    turning[6:8, :] = jnp.zeros((2, n_clump), F32)


def finish_kernel(
    n_shaft,
    n_lat,
    part_any,
    part,
    turning,
    centre,
    motion,
    inverse_mass,
    off,
    piece,
    route,
    clump,
    clump_out,
    sphere_out,
    got,
    table,
    hot_piece,
    hot_clump,
    pose,
    send_sem,
    recv_sem,
):
    place = Place(n_shaft, n_lat)
    n_piece, n_clump = route.shape[-1], part.shape[-1]

    def sums_copy(ds, dl, slot):
        c = (ds + 1) * 3 + dl + 1
        return pltpu.make_async_remote_copy(
            src_ref=part_any.at[c],
            dst_ref=got.at[slot],
            send_sem=send_sem.at[0, slot],
            recv_sem=recv_sem.at[0, slot],
            device_id=place.at(ds, dl),
            device_id_type=MESH,
        )

    def table_copy(ds, dl, slot):
        return pltpu.make_async_remote_copy(
            src_ref=table.at[4],
            dst_ref=table.at[slot],
            send_sem=send_sem.at[1, slot],
            recv_sem=recv_sem.at[1, slot],
            device_id=place.at(ds, dl),
            device_id_type=MESH,
        )

    def around(act, dl):
        for ds in (-1, 0, 1):
            if (ds, dl) != (0, 0):
                act(ds, dl)

    place.barrier()
    place.lateral(
        lambda dl: around(lambda ds, d: sums_copy(ds, d, (ds + 1) * 3 + d + 1).start(), dl)
    )

    def clear(edge, column):
        @pl.when(place.l == edge)
        def _():
            for row in range(3):
                table[row * 3 + column] = jnp.zeros((8, n_clump), F32)
                got[row * 3 + 2 - column] = jnp.zeros((8, n_clump), F32)

    clear(0, 0)
    clear(n_lat - 1, 2)
    for m in range(16):
        hot_piece[:, m * 128 : m * 128 + 128] = one_hot(
            n_piece, piece[0, :, m * 128 : m * 128 + 128]
        )
    for c in range(9):
        hot_clump[c * n_clump : (c + 1) * n_clump, :] = one_hot(
            n_clump, jnp.where(route[0] == c, clump[0], -1)
        )
    place.lateral(
        lambda dl: around(lambda ds, d: sums_copy(ds, d, 8 - (ds + 1) * 3 - d - 1).wait_recv(), dl)
    )
    sums = part[4]
    for c in range(9):
        if c != 4:
            sums = sums + got[c]
    rows = []
    for t in range(3):
        pull = -GRAVITY if t == 2 else 0.0
        rows.append(motion[t, 0] + TIME_STEP * (inverse_mass[0] * sums[t : t + 1] + pull))
    torque = [sums[3 + t : 4 + t] for t in range(3)]
    order = ((0, 1, 2), (1, 3, 4), (2, 4, 5))
    for t in range(3):
        change = sum(turning[order[t][i] : order[t][i] + 1, :] * torque[i] for i in range(3))
        rows.append(motion[3 + t, 0] + change)
    table[4] = jnp.concatenate(rows + [jnp.zeros((2, n_clump), F32)], 0)
    for t in range(3):
        clump_out[t, 0] = centre[t, 0] + TIME_STEP * rows[t]
    for t in range(6):
        clump_out[3 + t, 0] = rows[t]
    place.lateral(
        lambda dl: around(lambda ds, d: table_copy(ds, d, 8 - (ds + 1) * 3 - d - 1).start(), dl)
    )
    place.lateral(
        lambda dl: around(lambda ds, d: table_copy(ds, d, (ds + 1) * 3 + d + 1).wait_recv(), dl)
    )
    tables = jnp.concatenate([rows3(table[c]) for c in range(9)], 1)
    by_piece = lax.dot_general(tables, hot_clump[...], ROWS, preferred_element_type=F32)
    by_piece = by_piece.astype(BF16)
    by_sphere = sum3(
        lax.dot_general(by_piece, hot_piece[...], ROWS, preferred_element_type=F32)
    )
    for m in range(16):
        pose[m * 8 : m * 8 + 8, :] = by_sphere[:, m * 128 : m * 128 + 128]
    for j in range(2):
        vx, vy, vz, sx, sy, sz = (
            pose[pl.ds(j * 64 + t, 8, stride=8), :] for t in range(6)
        )
        bx, by, bz = (off[t, 0, j] for t in range(3))
        hx, hy, hz = (0.5 * TIME_STEP * s for s in (sx, sy, sz))
        scale = 2.0 / (1.0 + (hx * hx + hy * hy + hz * hz))
        cx, cy, cz = hy * bz - hz * by, hz * bx - hx * bz, hx * by - hy * bx
        tx = bx + scale * (cx + hy * cz - hz * cy)
        ty = by + scale * (cy + hz * cx - hx * cz)
        tz = bz + scale * (cz + hx * cy - hy * cx)
        sphere_out[0, 0, j], sphere_out[1, 0, j], sphere_out[2, 0, j] = tx, ty, tz
        sphere_out[3, 0, j] = vx + (sy * tz - sz * ty)
        sphere_out[4, 0, j] = vy + (sz * tx - sx * tz)
        sphere_out[5, 0, j] = vz + (sx * ty - sy * tx)
    place.lateral(
        lambda dl: around(lambda ds, d: sums_copy(ds, d, (ds + 1) * 3 + d + 1).wait_send(), dl)
    )
    place.lateral(
        lambda dl: around(lambda ds, d: table_copy(ds, d, 8 - (ds + 1) * 3 - d - 1).wait_send(), dl)
    )


def contact_call(lat_cells, blade_phase, ext, off, piece, route, clump, angles, inertia, **extra):
    n_clump = angles.shape[-1]
    return pl.pallas_call(
        functools.partial(contact_kernel, lat_cells),
        out_shape=(
            jax.ShapeDtypeStruct((9, 8, n_clump), F32),
            jax.ShapeDtypeStruct((8, n_clump), F32),
        ),
        in_specs=[SMEM] + [VMEM] * 7,
        out_specs=(VMEM, VMEM),
        scratch_shapes=[
            pltpu.VMEM((144, 128), jnp.int32),
            pltpu.VMEM((8, 512), jnp.int32),
            pltpu.SMEM((8, 512), jnp.int32),
            pltpu.SMEM((2, 16), jnp.int32),
            pltpu.VMEM((9, 256, 8), F32),
            pltpu.VMEM((9 * 1024 + 256, 8), F32),
            pltpu.VMEM((128, 128), F32),
            pltpu.SemaphoreType.DMA,
        ],
        compiler_params=pltpu.CompilerParams(vmem_limit_bytes=48 << 20),
        name="contact",
        **extra,
    )(blade_phase, ext, off, piece, route, clump, angles, inertia)


def on_device(
    n_shaft,
    n_lat,
    sphere_position,
    sphere_velocity,
    sphere_radius,
    sphere_offset,
    sphere_piece,
    piece_route,
    piece_clump,
    blade_phase,
    clump_centre,
    clump_motion,
    clump_angles,
    clump_inverse_mass,
    clump_inverse_inertia,
):
    n_piece, n_clump = piece_route.shape[-1], clump_angles.shape[-1]
    ext = pl.pallas_call(
        functools.partial(halo_kernel, n_shaft, n_lat),
        out_shape=jax.ShapeDtypeStruct((3, 4, 8, 8, 128), F32),
        in_specs=[ANY] * 3,
        out_specs=VMEM,
        scratch_shapes=[
            pltpu.SemaphoreType.DMA((3, 4, 3)),
            pltpu.SemaphoreType.DMA((3, 4, 3)),
            pltpu.SemaphoreType.DMA((2, 3)),
        ],
        compiler_params=pltpu.CompilerParams(collective_id=0, has_side_effects=True),
        name="halo",
    )(sphere_position, sphere_velocity, sphere_radius)
    part, turning = contact_call(
        2 * n_lat,
        blade_phase,
        ext.reshape(768, 128),
        sphere_offset,
        sphere_piece,
        piece_route,
        piece_clump,
        clump_angles,
        clump_inverse_inertia,
    )
    return pl.pallas_call(
        functools.partial(finish_kernel, n_shaft, n_lat),
        out_shape=(
            jax.ShapeDtypeStruct((9, 1, 1, n_clump), F32),
            jax.ShapeDtypeStruct((6, 1, 2, 8, 128), F32),
        ),
        in_specs=[ANY] + [VMEM] * 9,
        out_specs=(VMEM, VMEM),
        scratch_shapes=[
            pltpu.VMEM((9, 8, n_clump), F32),
            pltpu.VMEM((9, 8, n_clump), F32),
            pltpu.VMEM((n_piece, 2048), BF16),
            pltpu.VMEM((9 * n_clump, n_piece), BF16),
            pltpu.VMEM((128, 128), F32),
            pltpu.SemaphoreType.DMA((2, 9)),
            pltpu.SemaphoreType.DMA((2, 9)),
        ],
        compiler_params=pltpu.CompilerParams(
            collective_id=1, has_side_effects=True, vmem_limit_bytes=48 << 20
        ),
        name="finish",
    )(
        part,
        part,
        turning,
        clump_centre,
        clump_motion,
        clump_inverse_mass,
        sphere_offset,
        sphere_piece,
        piece_route,
        piece_clump,
    )


def solution(mesh):
    placed = (
        P(None, "shaft", "lat", None, None),
        P(None, "shaft", "lat", None, None),
        P("shaft", "lat", None, None),
        P(None, "shaft", "lat", None, None),
        P("shaft", "lat", None),
        P("shaft", "lat", None),
        P("shaft", "lat", None),
        P(),
        P(None, "shaft", "lat", None),
        P(None, "shaft", "lat", None),
        P(None, "shaft", "lat", None),
        P("shaft", "lat", None),
        P(None, "shaft", "lat", None),
    )
    return jax.shard_map(
        functools.partial(on_device, mesh.shape["shaft"], mesh.shape["lat"]),
        mesh=mesh,
        in_specs=placed,
        out_specs=(P(None, "shaft", "lat", None), P(None, "shaft", "lat", None, None)),
        check_vma=False,
    )
```

time: 629 us -> 93.9 us (0.15)
  other arithmetic: 450 us -> 0 us
  local copies, waits for them, and re-layouts: 113 us -> 2.9 us
  Pallas kernels: 0 us -> 89.8 us
  starting transfers between devices: 44 us -> 0 us
  waiting for transfers between devices: 15.8 us -> 0 us
    reduce_sum x22 -> x0, other arithmetic: 279 us -> none  [the longest x4 87.4 us: pair_force(): return jnp.sum(forces, 3)]
    pallas_call x0 -> x3, Pallas kernels: none -> 89.8 us  [the longest x1 54.3 us: contact_call(): pl.pallas_call(functools.partial(contact_kernel, lat_cells), out_shape=(j...]
    scatter x2 -> x0, local copies, waits for them, and re-layouts: 67.8 us -> none  [the longest x1 43.1 us: on_device(): jnp.full((9, capacity), clump_count, jnp.int32).at[codes, slots]]
    mul x14 -> x0, other arithmetic: 47.7 us -> none  [the longest x4 45.5 us: pair_force(): stiff_root * (STIFFNESS * intersection - NORMAL_DAMPING * normal_speed -...]
    ppermute x16 -> x0, starting transfers between devices: 44 us -> none  [the longest x6 19.2 us: shifted_3(): return lax.ppermute(x, axis, pairs)]
    div x12 -> x0, other arithmetic: 40.2 us -> none  [the longest x4 40.1 us: pair_force(): friction_cap / jnp.sqrt(jnp.sum(shear_force * shear_force, 0) + friction_...]
    max x4 -> x0, other arithmetic: 30.6 us -> none  [pair_force(): distance = jnp.maximum(distance, 0.25 * radius_sum)]
    scatter-add x2 -> x0, other arithmetic: 22.2 us -> none  [the longest x1 12.6 us: on_device(): jax.ops.segment_sum(terms.T, piece_ids, num_segments=piece_count, indices...]
  transfers between devices with their start and end apart: 16 -> 0, of which waited for: 7 -> 0; matrix products, arithmetic and copies ran while one was open for 9% -> 0% of each run, Pallas kernels for 0% -> 0%
where the time goes in v1:
time: 93.9 us; the launch traced here: 94.2 us
  Pallas kernels  89.8 us (96%)
  local copies, waits for them, and re-layouts  2.9 us (3%)
  between operations  1.43 us (2%)
    pallas_call x1, Pallas kernels, contact_call(): pl.pallas_call(functools.partial(contact_kernel, lat_cells), out_shape=(j...  54.3 us
    pallas_call x1, Pallas kernels, on_device(): pl.pallas_call(functools.partial(finish_kernel, n_shaft, n_lat), out_shap...  22.4 us
    pallas_call x1, Pallas kernels, on_device(): pl.pallas_call(functools.partial(halo_kernel, n_shaft, n_lat), out_shape=...  13.1 us
    unnamed x22, local copies, waits for them, and re-layouts  2.9 us

profile of v1, /device:TPU:1, one launch (start us, length us, event | category | flops | bytes accessed | tf_op | source)
XLA Modules:
  0.0 94.2 jit_solution(18036407300840143049)
XLA Ops:
  1.3 0.0 copy-start.1
  1.3 0.0 copy-start.2
  1.3 0.0 copy-start.3
  1.3 0.0 copy-start.4
  1.3 0.0 copy-start.6
  1.3 0.0 copy-start.7
  1.3 13.1 %halo.1 = f32[3,4,8,8,128]{4,3,2,1,0:T(8,128)} custom-call(f32[3,1,2,8,128]{4,3,2,1,0:T(8,128)} %pos.1, f32[3,1,2,8,128]{4,3,2,1,0:T(8,128)} %vel.1, f32[1,2,8,128]{3,2,1,0:T(8,128)} %rad.1), custom_call_target="tpu_custom_call" | custom-call | tf_op jit(solution)/shard_map/halo/pallas_call | solution.py:581
  14.4 0.0 copy-done.1
  14.5 0.0 copy-done.2
  14.5 0.0 copy-done.3
  14.5 0.0 copy-done.4
  14.5 0.0 copy-done.6
  14.5 0.0 copy-done.7
  14.5 0.0 copy-start
  14.5 1.0 %copy-done = f32[3,4,8,8,128]{4,3,2,1,0:T(8,128)S(1)} copy-done((f32[3,4,8,8,128]{4,3,2,1,0:T(8,128)S(1)}, f32[3,4,8,8,128]{4,3,2,1,0:T(8,128)}, u32[]{:S(2)}) %copy-start) | copy-done | bytes 393240
  15.5 0.0 copy-start.5
  15.5 0.0 copy-start.9
  15.5 54.3 %contact.1 = (f32[9,8,256]{2,1,0:T(8,128)S(1)}, f32[8,256]{1,0:T(8,128)S(1)}) custom-call(s32[1]{0:T(128)S(6)} %copy.17.phase, f32[768,128]{1,0:T(8,128)S(1)} %bitcast.1, f32[3,1,2,8,128]{4,3,2,1,0:T(8,128)S(1)} %copy-done.1, s32[1,1,2048]{2,1,0:T(1,128)S(1)} %copy-done.2, s32[1,1,512]{2,1,0:T(1,128)S(1)} %copy-done.3, s32[1,1,512]{2,1,0:T(1,128)S(1)} %copy-done.4, ...), custom_call_target="tpu_custom_call" | custom-call | tf_op jit(solution)/shard_map/contact/pallas_call | solution.py:539
  69.8 0.0 copy-start.8
  69.8 0.0 copy-done.5
  69.8 0.0 copy-done.9
  69.9 0.7 copy-done.8
  70.5 22.4 %finish.1 = (f32[9,1,1,256]{3,2,1,0:T(1,128)S(1)}, f32[6,1,2,8,128]{4,3,2,1,0:T(8,128)S(1)}) custom-call(f32[9,8,256]{2,1,0:T(8,128)S(1)} %get-tuple-element.4.part_any.part, f32[9,8,256]{2,1,0:T(8,128)S(1)} %get-tuple-element.4.part_any.part, f32[8,256]{1,0:T(8,128)S(1)} %get-tuple-element.5.turning, f32[3,1,1,256]{3,2,1,0:T(1,128)S(1)} %copy-done.8, ...), custom_call_target="tpu_custom_call" | custom-call | tf_op jit(solution)/shard_map/finish/pallas_call | solution.py:605
  92.9 0.6 copy.18
  93.6 0.6 copy.19
Async XLA Ops:
  1.3 13.2 %copy-start.1 = (f32[3,1,2,8,128]{4,3,2,1,0:T(8,128)S(1)}, f32[3,1,2,8,128]{4,3,2,1,0:T(8,128)}, u32[]{:S(2)}) copy-start(f32[3,1,2,8,128]{4,3,2,1,0:T(8,128)} %off.3) | copy-start | bytes 73732
  1.3 13.2 %copy-start.2 = (s32[1,1,2048]{2,1,0:T(1,128)S(1)}, s32[1,1,2048]{2,1,0:T(1,128)}, u32[]{:S(2)}) copy-start(s32[1,1,2048]{2,1,0:T(1,128)} %piece.3) | copy-start | bytes 24580
  1.3 13.2 %copy-start.3 = (s32[1,1,512]{2,1,0:T(1,128)S(1)}, s32[1,1,512]{2,1,0:T(1,128)}, u32[]{:S(2)}) copy-start(s32[1,1,512]{2,1,0:T(1,128)} %route.3) | copy-start | bytes 6148
  1.3 13.2 %copy-start.4 = (s32[1,1,512]{2,1,0:T(1,128)S(1)}, s32[1,1,512]{2,1,0:T(1,128)}, u32[]{:S(2)}) copy-start(s32[1,1,512]{2,1,0:T(1,128)} %clump.3) | copy-start | bytes 6148
  1.3 13.2 %copy-start.6 = (f32[3,1,1,256]{3,2,1,0:T(1,128)S(1)}, f32[3,1,1,256]{3,2,1,0:T(1,128)}, u32[]{:S(2)}) copy-start(f32[3,1,1,256]{3,2,1,0:T(1,128)} %angles.1) | copy-start | bytes 9220
  1.3 13.2 %copy-start.7 = (f32[3,1,1,256]{3,2,1,0:T(1,128)S(1)}, f32[3,1,1,256]{3,2,1,0:T(1,128)}, u32[]{:S(2)}) copy-start(f32[3,1,1,256]{3,2,1,0:T(1,128)} %inertia.1) | copy-start | bytes 9220
  14.5 1.0 %copy-start = (f32[3,4,8,8,128]{4,3,2,1,0:T(8,128)S(1)}, f32[3,4,8,8,128]{4,3,2,1,0:T(8,128)}, u32[]{:S(2)}) copy-start(f32[3,4,8,8,128]{4,3,2,1,0:T(8,128)} %halo.1) | copy-start | bytes 1179652
  15.5 54.3 %copy-start.5 = (f32[6,1,1,256]{3,2,1,0:T(1,128)S(1)}, f32[6,1,1,256]{3,2,1,0:T(1,128)}, u32[]{:S(2)}) copy-start(f32[6,1,1,256]{3,2,1,0:T(1,128)} %motion.1) | copy-start | bytes 18436
  15.5 54.3 %copy-start.9 = (f32[1,1,256]{2,1,0:T(1,128)S(1)}, f32[1,1,256]{2,1,0:T(1,128)}, u32[]{:S(2)}) copy-start(f32[1,1,256]{2,1,0:T(1,128)} %inverse_mass.1) | copy-start | bytes 3076
  69.8 0.7 copy-start.8

commit v2 on v1

--- a/solution.py
+++ b/solution.py
@@ -80,7 +80,22 @@
         pl.semaphore_wait(sem, jnp.where(edge, 5, 8))
 
 
-def halo_kernel(n_shaft, n_lat, pos, vel, rad, ext, send_sem, recv_sem, own_sem):
+def halo_kernel(
+    n_shaft,
+    n_lat,
+    pos,
+    vel,
+    rad,
+    piece,
+    route,
+    clump,
+    ext,
+    hot_piece,
+    hot_clump,
+    send_sem,
+    recv_sem,
+    own_sem,
+):
     place = Place(n_shaft, n_lat)
 
     def parts(j, si, lj):
@@ -139,32 +154,87 @@
     def _():
         ext[:, 3, 0:7] = jnp.zeros((3, 7, 8, 128), F32)
 
+    for m in range(16):
+        hot_piece[:, m * 128 : m * 128 + 128] = one_hot(
+            hot_piece.shape[0], piece[0, :, m * 128 : m * 128 + 128]
+        )
+    n_clump = hot_clump.shape[0] // 9
+    for c in range(9):
+        hot_clump[c * n_clump : (c + 1) * n_clump, :] = one_hot(
+            n_clump, jnp.where(route[0] == c, clump[0], -1)
+        )
     for c in own:
         c.wait()
     place.lateral(lambda dl: [c.wait_recv() for c in incoming(dl)] and None)
     place.lateral(lambda dl: [c.wait_send() for c in outgoing(dl)] and None)
 
 
-def pair_sums(mine, other, acc):
-    ax, ay, az, au, av, aw, ar, ar4 = mine
-    bx, by, bz, bu, bv, bw, br = other
-    dx, dy, dz = ax - bx, ay - by, az - bz
+USUAL = {0: (128, 64, 96, 64), 1: (64, 24, 40, 24), 2: (32, 16, 24, 16)}
+KEYS = 32
+TERMS = 9
+
+
+def kind(c):
+    return (c // 3 != 1) + (c % 3 != 1)
+
+
+def keyed(value, sub):
+    radius = value[6:7]
+    value = jnp.where(sub == 7, radius * radius * 0.0625, value)
+    high = value.astype(BF16).astype(F32)
+    rest = value - high
+    middle = rest.astype(BF16).astype(F32)
+    more = jnp.where(
+        sub < 3,
+        1.0,
+        jnp.where(sub < 5, high[6:7], jnp.where(sub == 5, middle[6:7], 0.0)),
+    )
+    return jnp.concatenate([high, middle, rest - middle, more], 0).astype(BF16)
+
+
+def own_table(own, sub, table):
+    zero = jnp.zeros((8, 128), F32)
+
+    def split(row):
+        return [p.astype(F32) for p in split3(jnp.broadcast_to(row, (8, 128)))]
+
+    def constants(row):
+        high, middle, low = split(row)
+        return jnp.where(sub == 0, high, jnp.where(sub == 1, middle, jnp.where(sub == 2, low, 0.0)))
+
+    def put(t, same, more):
+        block = jnp.concatenate([same, same, same, more], 0)
+        table[:, t * 128 : t * 128 + 128] = block.astype(BF16)
+
+    for t in range(7):
+        put(t, jnp.where(sub == t, 1.0 if t == 6 else -1.0, zero), constants(own[t]))
+    high, middle, low = split(4.0 * own[6])
+    same = jnp.where(sub == 6, high, 0.0)
+    more = jnp.where(sub == 4, low, jnp.where((sub == 3) | (sub == 5), middle, 0.0))
+    put(7, same, more)
+    put(
+        8,
+        jnp.where(sub == 7, 1.0, same * 0.03125),
+        more * 0.03125 + constants(own[6] * own[6] * 0.0625),
+    )
+
+
+def pair_sums(pair, acc):
+    dx, dy, dz, du, dv, dw, radii, product, least = pair
     square = dx * dx + dy * dy + dz * dz
-    radii = ar + br
-    clamped = jnp.maximum(square, radii * radii * 0.0625)
+    clamped = jnp.maximum(square, least)
     inverse = lax.rsqrt(clamped)
     delta = jnp.maximum(radii - clamped * inverse, 0.0)
-    du, dv, dw = au - bu, av - bv, aw - bw
     normal_speed = (du * dx + dv * dy + dw * dz) * inverse
     speed = du * du + dv * dv + dw * dw
     unit = square * (inverse * inverse)
-    sliding = jnp.maximum(speed + normal_speed * normal_speed * (unit - 2.0), 0.0)
-    load = ar4 * br * delta
+    sliding = speed + normal_speed * normal_speed * (unit - 2.0)
+    load = product * delta
     root = load * lax.rsqrt(jnp.maximum(load * radii, 1e-30))
     root2 = root * root
     cap = 2.5 * delta
-    shear = root2 * cap * lax.rsqrt(root2 * (sliding + cap * cap) + 1e-06)
-    push = root * (5.0 * delta - normal_speed - 0.25)
+    shear = root2 * cap * lax.rsqrt(jnp.maximum(root2 * (sliding + cap * cap), 0.0) + 1e-06)
+    push = root * (cap + cap - normal_speed - 0.25)
     along = (push + shear * normal_speed) * inverse
     return (
         acc[0] + (along * dx - shear * du),
@@ -178,9 +248,8 @@
     phase,
     ext,
     off,
-    piece,
-    route,
-    clump,
+    hot_piece,
+    hot_clump,
     angles,
     inertia,
     part,
@@ -191,6 +260,9 @@
     bounds,
     picked,
     packed,
+    table,
+    pairs_a,
+    pairs_b,
     force,
     copy_sem,
 ):
@@ -219,16 +291,16 @@
             low_f = jnp.where(low, kept, 0.0)
             high_f = jnp.where(high, kept, 0.0)
             masks += [low_f, kept - low_f - high_f, high_f]
-        mask_f = jnp.concatenate(masks, 0)
-        mask = mask_f.astype(BF16)
+        mask = jnp.concatenate(masks, 0).astype(BF16)
         prefix = lax.dot_general(mask, before, ROWS, preferred_element_type=F32)
         total = lax.dot_general(mask, ones, ROWS, preferred_element_type=F32)
         counts = lax.dot_general(ones[0:8], mask, LANES, preferred_element_type=F32)
-        count_v[:, j * 256 : j * 256 + 216] = counts.astype(jnp.int32)
+        count_v[0:8, j * 256 : j * 256 + 216] = counts.astype(jnp.int32)
+        over = jnp.full((8, 128), -1.0, F32)
         for c in range(9):
             a = c * 24
             low_p, mid_p, high_p = (prefix[a + 8 * t : a + 8 * t + 8] for t in range(3))
-            low_n, mid_n = total[a : a + 8], total[a + 8 : a + 16]
+            low_n, mid_n, high_n = (total[a + 8 * t : a + 8 * t + 8] for t in range(3))
             spot = (
                 masks[3 * c] * low_p
                 + masks[3 * c + 1] * (low_n + mid_p)
@@ -237,16 +309,20 @@
             any_of = masks[3 * c] + masks[3 * c + 1] + masks[3 * c + 2]
             spot = jnp.where(any_of > 0.0, spot, -1.0).astype(jnp.int32)
             dest[(j * 9 + c) * 8 : (j * 9 + c) * 8 + 8, :] = spot
+            sizes = (low_n + mid_n + high_n, low_n, mid_n, high_n)
+            for size, usual in zip(sizes, USUAL[kind(c)]):
+                over = jnp.maximum(over, size - usual)
+        count_v[8:16, j * 128 : j * 128 + 128] = over.astype(jnp.int32)
     copy = pltpu.make_async_copy(count_v, count_s, copy_sem)
     copy.start()
     copy.wait()
 
     for j in range(2):
 
-        def count(c, part_id, k):
-            return count_s[0, j * 256 + (c * 3 + part_id) * 8 + k]
-
-        def gather_level(k, offset):
+        def count(c, t, k):
+            return count_s[0, j * 256 + (c * 3 + t) * 8 + k]
+
+        def gather_level(k, offset, sizes):
             rise = CELL_SIDE * k.astype(F32) - 20.0
             for c in range(9):
                 di, dj = c // 3 - 1, c % 3 - 1
@@ -257,49 +333,38 @@
                     CELL_SIDE * di,
                     jnp.where(sub == 1, CELL_SIDE * dj, jnp.where(sub == 2, rise, 0.0)),
                 )
-                value = jnp.concatenate(split3(value + shift), 1)
                 spot = dest[pl.ds((j * 9 + c) * 8 + k, 1), :]
-
-                def pick(first, last):
-                    ids = lax.broadcasted_iota(jnp.int32, (last - first, 128), 0) + first
-                    hot = jnp.where(ids == spot, 1.0, 0.0).astype(BF16)
-                    picked[c, first:last, :] = lax.dot_general(
-                        jnp.concatenate([hot, hot, hot], 1),
-                        value,
-                        LANES,
-                        preferred_element_type=F32,
-                    )
-
-                if c == 4:
-                    pick(0, 128)
-                else:
-                    pick(0, 64)
-                    full = count(c, 0, k) + count(c, 1, k) + count(c, 2, k)
-                    pl.when(full > 64)(lambda: pick(64, 128))
+                rows = sizes[kind(c)][0]
+                picked[c, 0:rows, :] = lax.dot_general(
+                    one_hot(rows, spot),
+                    keyed(value + shift, sub),
+                    LANES,
+                    preferred_element_type=F32,
+                )
             for t in range(3):
                 if t == 2:
                     bounds[0, k] = offset
                 for c in range(9):
-                    amount = count(c, t, k)
                     start = 0 if t == 0 else count(c, 0, k)
                     if t == 2:
                         start = start + count(c, 1, k)
-                    short = (64 if t != 1 else 96) if c == 4 else 32
-
-                    def move(first, length):
-                        packed[pl.ds(offset + first, length), :] = picked[
-                            c, pl.ds(start + first, length), :
-                        ]
-
-                    move(0, short)
-                    pl.when(amount > short)(lambda: move(short, 128 - short))
-                    offset = offset + amount
+                    length = sizes[kind(c)][1 + t]
+                    packed[pl.ds(offset, length), :] = picked[c, pl.ds(start, length), :]
+                    offset = offset + count(c, t, k)
                 if t == 0:
                     bounds[1, k] = offset
             return offset
 
-        end = lax.fori_loop(0, 8, gather_level, jnp.int32(0))
-        packed[pl.ds(end, 64), :] = jnp.zeros((64, 8), F32)
+        def level(k, offset):
+            return lax.cond(
+                count_s[8 + k, j * 128] > 0,
+                lambda: gather_level(k, offset, {t: (128,) * 4 for t in range(3)}),
+                lambda: gather_level(k, offset, USUAL),
+            )
+
+        end = lax.fori_loop(0, 8, level, jnp.int32(0))
+        lane = lax.broadcasted_iota(jnp.int32, (64, KEYS), 1)
+        packed[pl.ds(end, 64), :] = jnp.where((lane >= 24) & (lane < 27), 1.0, 0.0)
         bounds[1, 8] = end
 
         def cell(k, _):
@@ -307,22 +372,38 @@
             base = (5 + j) * 64
             own = [ext[pl.ds(base + 8 * t + k, 1), :] for t in range(7)]
             own[2] = own[2] + rise
-            own.append(4.0 * own[6])
-            own = [jnp.broadcast_to(v, (8, 128)) for v in own]
+            own_table(own, sub, table)
             first = jnp.where(k == 0, 0, bounds[0, jnp.maximum(k - 1, 0)])
             first = (first // 8) * 8
             last = bounds[1, k + 1]
 
-            def chunk(i, acc):
+            def fill(i, pairs):
+                at = pl.multiple_of(first + i * CHUNK, 8)
+                pairs[...] = lax.dot_general(
+                    packed[pl.ds(at, CHUNK), :].astype(BF16),
+                    table[...],
+                    ROWS,
+                    preferred_element_type=F32,
+                )
+
+            def use(pairs, acc):
                 for g in range(CHUNK // 8):
-                    at = pl.multiple_of(first + i * CHUNK + g * 8, 8)
-                    rows = packed[pl.ds(at, 8), :]
-                    acc = pair_sums(own, [rows[:, t : t + 1] for t in range(7)], acc)
+                    pair = [
+                        pairs[g * 8 : g * 8 + 8, t * 128 : t * 128 + 128] for t in range(TERMS)
+                    ]
+                    acc = pair_sums(pair, acc)
                 return acc
 
+            def chunks(i, acc):
+                fill(2 * i + 1, pairs_b)
+                acc = use(pairs_a, acc)
+                fill(2 * i + 2, pairs_a)
+                return use(pairs_b, acc)
+
+            fill(0, pairs_a)
             zero = jnp.zeros((8, 128), F32)
             sums = lax.fori_loop(
-                0, (last - first + CHUNK - 1) // CHUNK, chunk, (zero, zero, zero)
+                0, (last - first + 2 * CHUNK - 1) // (2 * CHUNK), chunks, (zero, zero, zero)
             )
             for t in range(3):
                 force[pl.ds((j * 8 + t) * 8 + k, 1), :] = jnp.sum(sums[t], 0, keepdims=True)
@@ -362,23 +443,15 @@
             )
         for k in range(8):
             terms.append(rows3(force[pl.ds(j * 64 + k, 8, stride=8), :]))
-    n_piece = route.shape[-1]
-    sums = jnp.zeros((24, n_piece), F32)
-    for pair in range(8):
-        row = piece[0, :, pair * 256 : pair * 256 + 256]
-        sums = sums + lax.dot_general(
-            jnp.concatenate([terms[2 * pair], terms[2 * pair + 1]], 1),
-            one_hot(n_piece, row),
-            LANES,
-            preferred_element_type=F32,
-        )
-    sums = rows3(sum3(sums))
+    sums = lax.dot_general(
+        jnp.concatenate(terms, 1), hot_piece[...], LANES, preferred_element_type=F32
+    )
+    sums = sum3(
+        lax.dot_general(rows3(sum3(sums)), hot_clump[...], LANES, preferred_element_type=F32)
+    )
     n_clump = part.shape[-1]
     for c in range(9):
-        key = jnp.where(route[0] == c, clump[0], -1)
-        part[c] = sum3(
-            lax.dot_general(sums, one_hot(n_clump, key), LANES, preferred_element_type=F32)
-        )
+        part[c] = sums[:, c * n_clump : (c + 1) * n_clump]
 
     cos_z, cos_y, cos_x = (jnp.cos(angles[t, 0]) for t in range(3))
     sin_z, sin_y, sin_x = (jnp.sin(angles[t, 0]) for t in range(3))
@@ -412,21 +485,18 @@
     motion,
     inverse_mass,
     off,
-    piece,
-    route,
-    clump,
+    hot_piece,
+    hot_clump,
     clump_out,
     sphere_out,
     got,
     table,
-    hot_piece,
-    hot_clump,
     pose,
     send_sem,
     recv_sem,
 ):
     place = Place(n_shaft, n_lat)
-    n_piece, n_clump = route.shape[-1], part.shape[-1]
+    n_clump = part.shape[-1]
 
     def sums_copy(ds, dl, slot):
         c = (ds + 1) * 3 + dl + 1
@@ -468,14 +538,6 @@
 
     clear(0, 0)
     clear(n_lat - 1, 2)
-    for m in range(16):
-        hot_piece[:, m * 128 : m * 128 + 128] = one_hot(
-            n_piece, piece[0, :, m * 128 : m * 128 + 128]
-        )
-    for c in range(9):
-        hot_clump[c * n_clump : (c + 1) * n_clump, :] = one_hot(
-            n_clump, jnp.where(route[0] == c, clump[0], -1)
-        )
     place.lateral(
         lambda dl: around(lambda ds, d: sums_copy(ds, d, 8 - (ds + 1) * 3 - d - 1).wait_recv(), dl)
     )
@@ -534,7 +596,7 @@
     )
 
 
-def contact_call(lat_cells, blade_phase, ext, off, piece, route, clump, angles, inertia, **extra):
+def contact_call(lat_cells, blade_phase, ext, off, hot_piece, hot_clump, angles, inertia, **extra):
     n_clump = angles.shape[-1]
     return pl.pallas_call(
         functools.partial(contact_kernel, lat_cells),
@@ -542,22 +604,25 @@
             jax.ShapeDtypeStruct((9, 8, n_clump), F32),
             jax.ShapeDtypeStruct((8, n_clump), F32),
         ),
-        in_specs=[SMEM] + [VMEM] * 7,
+        in_specs=[SMEM] + [VMEM] * 6,
         out_specs=(VMEM, VMEM),
         scratch_shapes=[
             pltpu.VMEM((144, 128), jnp.int32),
-            pltpu.VMEM((8, 512), jnp.int32),
-            pltpu.SMEM((8, 512), jnp.int32),
+            pltpu.VMEM((16, 512), jnp.int32),
+            pltpu.SMEM((16, 512), jnp.int32),
             pltpu.SMEM((2, 16), jnp.int32),
-            pltpu.VMEM((9, 256, 8), F32),
-            pltpu.VMEM((9 * 1024 + 256, 8), F32),
+            pltpu.VMEM((9, 256, KEYS), F32),
+            pltpu.VMEM((9 * 1024 + 256, KEYS), F32),
+            pltpu.VMEM((KEYS, TERMS * 128), BF16),
+            pltpu.VMEM((CHUNK, TERMS * 128), F32),
+            pltpu.VMEM((CHUNK, TERMS * 128), F32),
             pltpu.VMEM((128, 128), F32),
             pltpu.SemaphoreType.DMA,
         ],
-        compiler_params=pltpu.CompilerParams(vmem_limit_bytes=48 << 20),
+        compiler_params=pltpu.CompilerParams(vmem_limit_bytes=20 << 20),
         name="contact",
         **extra,
-    )(blade_phase, ext, off, piece, route, clump, angles, inertia)
+    )(blade_phase, ext, off, hot_piece, hot_clump, angles, inertia)
 
 
 def on_device(
@@ -578,27 +643,39 @@
     clump_inverse_inertia,
 ):
     n_piece, n_clump = piece_route.shape[-1], clump_angles.shape[-1]
-    ext = pl.pallas_call(
+    ext, hot_piece, hot_clump = pl.pallas_call(
         functools.partial(halo_kernel, n_shaft, n_lat),
-        out_shape=jax.ShapeDtypeStruct((3, 4, 8, 8, 128), F32),
-        in_specs=[ANY] * 3,
-        out_specs=VMEM,
+        out_shape=(
+            jax.ShapeDtypeStruct((3, 4, 8, 8, 128), F32),
+            jax.ShapeDtypeStruct((n_piece, 2048), BF16),
+            jax.ShapeDtypeStruct((9 * n_clump, n_piece), BF16),
+        ),
+        in_specs=[ANY] * 3 + [VMEM] * 3,
+        out_specs=(VMEM,) * 3,
         scratch_shapes=[
             pltpu.SemaphoreType.DMA((3, 4, 3)),
             pltpu.SemaphoreType.DMA((3, 4, 3)),
             pltpu.SemaphoreType.DMA((2, 3)),
         ],
-        compiler_params=pltpu.CompilerParams(collective_id=0, has_side_effects=True),
+        compiler_params=pltpu.CompilerParams(
+            collective_id=0, has_side_effects=True, vmem_limit_bytes=16 << 20
+        ),
         name="halo",
-    )(sphere_position, sphere_velocity, sphere_radius)
+    )(
+        sphere_position,
+        sphere_velocity,
+        sphere_radius,
+        sphere_piece,
+        piece_route,
+        piece_clump,
+    )
     part, turning = contact_call(
         2 * n_lat,
         blade_phase,
         ext.reshape(768, 128),
         sphere_offset,
-        sphere_piece,
-        piece_route,
-        piece_clump,
+        hot_piece,
+        hot_clump,
         clump_angles,
         clump_inverse_inertia,
     )
@@ -608,19 +685,17 @@
             jax.ShapeDtypeStruct((9, 1, 1, n_clump), F32),
             jax.ShapeDtypeStruct((6, 1, 2, 8, 128), F32),
         ),
-        in_specs=[ANY] + [VMEM] * 9,
+        in_specs=[ANY] + [VMEM] * 8,
         out_specs=(VMEM, VMEM),
         scratch_shapes=[
             pltpu.VMEM((9, 8, n_clump), F32),
             pltpu.VMEM((9, 8, n_clump), F32),
-            pltpu.VMEM((n_piece, 2048), BF16),
-            pltpu.VMEM((9 * n_clump, n_piece), BF16),
             pltpu.VMEM((128, 128), F32),
             pltpu.SemaphoreType.DMA((2, 9)),
             pltpu.SemaphoreType.DMA((2, 9)),
         ],
         compiler_params=pltpu.CompilerParams(
-            collective_id=1, has_side_effects=True, vmem_limit_bytes=48 << 20
+            collective_id=1, has_side_effects=True, vmem_limit_bytes=16 << 20
         ),
         name="finish",
     )(
@@ -631,9 +706,8 @@
         clump_motion,
         clump_inverse_mass,
         sphere_offset,
-        sphere_piece,
-        piece_route,
-        piece_clump,
+        hot_piece,
+        hot_clump,
     )
 
 

time: 93.9 us -> 77 us (0.82); the launches traced: 94.2 us -> 76.1 us
  Pallas kernels: 89.8 us -> 67.1 us
  local copies, waits for them, and re-layouts: 2.9 us -> 7.55 us
    pallas_call x1, Pallas kernels: 54.3 us -> 33.8 us  [contact_call(): pl.pallas_call(functools.partial(contact_kernel, lat_cells), out_shape=(j...]
    unnamed x22 -> x26, local copies, waits for them, and re-layouts: 2.9 us -> 7.55 us
    pallas_call x1, Pallas kernels: 13.1 us -> 12 us  [on_device(): pl.pallas_call(functools.partial(halo_kernel, n_shaft, n_lat), out_shape=...]
    pallas_call x1, Pallas kernels: 22.4 us -> 21.4 us  [on_device(): pl.pallas_call(functools.partial(finish_kernel, n_shaft, n_lat), out_shap...]
where the time goes in v2:
time: 77 us; the launch traced here: 76.1 us
  Pallas kernels  67.1 us (87%)
  local copies, waits for them, and re-layouts  7.55 us (10%)
  between operations  1.35 us (2%)
    pallas_call x1, Pallas kernels, contact_call(): pl.pallas_call(functools.partial(contact_kernel, lat_cells), out_shape=(j...  33.8 us
    pallas_call x1, Pallas kernels, on_device(): pl.pallas_call(functools.partial(finish_kernel, n_shaft, n_lat), out_shap...  21.4 us
    pallas_call x1, Pallas kernels, on_device(): pl.pallas_call(functools.partial(halo_kernel, n_shaft, n_lat), out_shape=...  12 us
    unnamed x26, local copies, waits for them, and re-layouts  7.55 us

profile of v2, /device:TPU:1, one launch (start us, length us, event | category | flops | bytes accessed | tf_op | source)
XLA Modules:
  0.0 76.1 jit_solution(4626485756537719715)
XLA Ops:
  1.3 0.0 copy-start.1
  1.3 0.7 copy-done.1
  2.0 0.0 copy-start.2
  2.0 0.7 copy-done.2
  2.8 0.0 copy-start.3
  2.8 0.7 copy-done.3
  3.5 0.0 copy-start.4
  3.5 0.7 copy-done.4
  4.2 0.0 copy-start.9
  4.2 0.7 copy-done.9
  4.8 0.0 copy-start.10
  4.8 0.7 copy-done.10
  5.5 12.0 %halo.1 = (f32[3,4,8,8,128]{4,3,2,1,0:T(8,128)S(1)}, bf16[512,2048]{1,0:T(8,128)(2,1)S(1)}, bf16[2304,512]{1,0:T(8,128)(2,1)S(1)}) custom-call(f32[3,1,2,8,128]{4,3,2,1,0:T(8,128)S(1)} %copy-done.1, f32[3,1,2,8,128]{4,3,2,1,0:T(8,128)S(1)} %copy-done.2, f32[1,2,8,128]{3,2,1,0:T(8,128)S(1)} %copy-done.3, s32[1,1,2048]{2,1,0:T(1,128)S(1)} %copy-done.4, ...), custom_call_target="tpu_custom_call" | custom-call | tf_op jit(solution)/shard_map/halo/pallas_call | solution.py:646
  17.5 0.0 copy-start
  17.5 0.7 copy-done
  18.2 0.0 copy-start.6
  18.2 0.7 copy-done.6
  18.9 0.0 copy-start.7
  18.9 0.7 copy-done.7
  19.6 0.0 copy-start.5
  19.6 0.0 copy-start.8
  19.6 0.0 copy-start.11
  19.6 33.8 %contact.1 = (f32[9,8,256]{2,1,0:T(8,128)S(1)}, f32[8,256]{1,0:T(8,128)S(1)}) custom-call(s32[1]{0:T(128)S(6)} %copy.17.phase, f32[768,128]{1,0:T(8,128)S(1)} %bitcast.1, f32[3,1,2,8,128]{4,3,2,1,0:T(8,128)S(1)} %copy-done, bf16[512,2048]{1,0:T(8,128)(2,1)S(1)} %get-tuple-element.8.hot_piece, bf16[2304,512]{1,0:T(8,128)(2,1)S(1)} %get-tuple-element.9.hot_clump, ...), custom_call_target="tpu_custom_call" | custom-call | tf_op jit(solution)/shard_map/contact/pallas_call | solution.py:601
  53.4 0.0 copy-done.5
  53.4 0.0 copy-done.8
  53.5 0.0 copy-done.11
  53.5 21.4 %finish.1 = (f32[9,1,1,256]{3,2,1,0:T(1,128)S(1)}, f32[6,1,2,8,128]{4,3,2,1,0:T(8,128)S(1)}) custom-call(f32[9,8,256]{2,1,0:T(8,128)S(1)} %get-tuple-element.10.part_any.part, f32[9,8,256]{2,1,0:T(8,128)S(1)} %get-tuple-element.10.part_any.part, f32[8,256]{1,0:T(8,128)S(1)} %get-tuple-element.11.turning, f32[3,1,1,256]{3,2,1,0:T(1,128)S(1)} %copy-done.8, ...), custom_call_target="tpu_custom_call" | custom-call | tf_op jit(solution)/shard_map/finish/pallas_call | solution.py:682
  74.8 0.6 copy.18
  75.4 0.6 copy.19
Async XLA Ops:
  1.3 0.7 copy-start.1
  2.0 0.7 copy-start.2
  2.8 0.7 copy-start.3
  3.5 0.7 copy-start.4
  4.2 0.7 copy-start.9
  4.8 0.7 copy-start.10
  17.5 0.7 copy-start
  18.2 0.7 copy-start.6
  18.9 0.7 copy-start.7
  19.6 33.8 %copy-start.5 = (f32[6,1,1,256]{3,2,1,0:T(1,128)S(1)}, f32[6,1,1,256]{3,2,1,0:T(1,128)}, u32[]{:S(2)}) copy-start(f32[6,1,1,256]{3,2,1,0:T(1,128)} %motion.1) | copy-start | bytes 18436
  19.6 33.8 %copy-start.8 = (f32[3,1,1,256]{3,2,1,0:T(1,128)S(1)}, f32[3,1,1,256]{3,2,1,0:T(1,128)}, u32[]{:S(2)}) copy-start(f32[3,1,1,256]{3,2,1,0:T(1,128)} %centre.1) | copy-start | bytes 9220
  19.6 33.8 %copy-start.11 = (f32[1,1,256]{2,1,0:T(1,128)S(1)}, f32[1,1,256]{2,1,0:T(1,128)}, u32[]{:S(2)}) copy-start(f32[1,1,256]{2,1,0:T(1,128)} %inverse_mass.1) | copy-start | bytes 3076

commit v3 on v2

--- a/solution.py
+++ b/solution.py
@@ -24,7 +24,7 @@
 ROWS = (((1,), (0,)), ((), ()))
 VMEM = pl.BlockSpec(memory_space=pltpu.VMEM)
 SMEM = pl.BlockSpec(memory_space=pltpu.SMEM)
-ANY = pl.BlockSpec(memory_space=pl.ANY)
+HBM = pl.BlockSpec(memory_space=pltpu.HBM)
 
 
 def split3(x):
@@ -86,15 +86,23 @@
     pos,
     vel,
     rad,
+    piece_hbm,
+    route_hbm,
+    clump_hbm,
+    ext,
+    hot_piece,
+    hot_clump,
+    inside,
     piece,
     route,
     clump,
-    ext,
-    hot_piece,
-    hot_clump,
+    table,
+    pairs_a,
+    pairs_b,
     send_sem,
     recv_sem,
     own_sem,
+    load_sem,
 ):
     place = Place(n_shaft, n_lat)
 
@@ -140,10 +148,16 @@
         for j in (0, 1)
         for t, (src, dst) in enumerate(parts(j, 1, 1 + j))
     ]
+    own += [
+        pltpu.make_async_copy(src, dst, load_sem.at[t])
+        for t, (src, dst) in enumerate(
+            ((piece_hbm, piece), (route_hbm, route), (clump_hbm, clump))
+        )
+    ]
+    for c in own:
+        c.start()
     place.barrier()
     place.lateral(lambda dl: [c.start() for c in outgoing(dl)] and None)
-    for c in own:
-        c.start()
     ext[:, :, 7] = jnp.zeros((3, 4, 8, 128), F32)
 
     @pl.when(place.l == 0)
@@ -154,6 +168,29 @@
     def _():
         ext[:, 3, 0:7] = jnp.zeros((3, 7, 8, 128), F32)
 
+    for c in own:
+        c.wait()
+    sub = lax.broadcasted_iota(jnp.int32, (8, 128), 0)
+    every = one_hot(128, lax.broadcasted_iota(jnp.int32, (1, 128), 1))
+    inside[...] = jnp.zeros((128, 128), F32)
+
+    def cell(m, _):
+        j, k = m // 8, m % 8
+        mine = [ext[1, 1 + j, t, pl.ds(k, 1), :] for t in range(7)]
+        own_table(mine, sub, table)
+        value = jnp.concatenate(mine + [mine[6]], 0)
+        rows = lax.dot_general(every, keyed(value, sub), LANES, preferred_element_type=F32)
+        zero = jnp.zeros((8, 128), F32)
+        acc = (zero, zero, zero)
+        for i in range(128 // CHUNK):
+            pairs = (pairs_a, pairs_b)[i % 2]
+            fill(rows[i * CHUNK : (i + 1) * CHUNK], table, pairs)
+            acc = use(pairs, acc)
+        for t in range(3):
+            inside[pl.ds((j * 8 + t) * 8 + k, 1), :] = jnp.sum(acc[t], 0, keepdims=True)
+        return 0
+
+    lax.fori_loop(0, 16, cell, 0)
     for m in range(16):
         hot_piece[:, m * 128 : m * 128 + 128] = one_hot(
             hot_piece.shape[0], piece[0, :, m * 128 : m * 128 + 128]
@@ -163,13 +200,11 @@
         hot_clump[c * n_clump : (c + 1) * n_clump, :] = one_hot(
             n_clump, jnp.where(route[0] == c, clump[0], -1)
         )
-    for c in own:
-        c.wait()
     place.lateral(lambda dl: [c.wait_recv() for c in incoming(dl)] and None)
     place.lateral(lambda dl: [c.wait_send() for c in outgoing(dl)] and None)
 
 
-USUAL = {0: (128, 64, 96, 64), 1: (64, 24, 40, 24), 2: (32, 16, 24, 16)}
+USUAL = {0: (128, 64, 64, 64), 1: (64, 24, 40, 24), 2: (32, 16, 24, 16)}
 KEYS = 32
 TERMS = 9
 
@@ -243,22 +278,41 @@
     )
 
 
+def fill(rows, table, pairs):
+    pairs[...] = lax.dot_general(
+        rows.astype(BF16), table[...], ROWS, preferred_element_type=F32
+    )
+
+
+def use(pairs, acc):
+    for g in range(CHUNK // 8):
+        acc = pair_sums(
+            [pairs[g * 8 : g * 8 + 8, t * 128 : t * 128 + 128] for t in range(TERMS)], acc
+        )
+    return acc
+
+
 def contact_kernel(
     lat_cells,
     phase,
     ext,
-    off,
     hot_piece,
     hot_clump,
+    inside,
+    off_hbm,
+    angles_hbm,
+    inertia_hbm,
+    part,
+    turning,
+    off,
     angles,
     inertia,
-    part,
-    turning,
     dest,
     count_v,
     count_s,
     bounds,
     picked,
+    picked_own,
     packed,
     table,
     pairs_a,
@@ -266,6 +320,14 @@
     force,
     copy_sem,
 ):
+    loads = [
+        pltpu.make_async_copy(src, dst, copy_sem.at[1 + t])
+        for t, (src, dst) in enumerate(
+            ((angles_hbm, angles), (inertia_hbm, inertia), (off_hbm, off))
+        )
+    ]
+    for load in loads:
+        load.start()
     sub = lax.broadcasted_iota(jnp.int32, (8, 128), 0)
 
     before = jnp.where(
@@ -290,7 +352,8 @@
             kept = jnp.where(keep, 1.0, 0.0)
             low_f = jnp.where(low, kept, 0.0)
             high_f = jnp.where(high, kept, 0.0)
-            masks += [low_f, kept - low_f - high_f, high_f]
+            mid_f = jnp.zeros((8, 128), F32) if c == 4 else kept - low_f - high_f
+            masks += [low_f, mid_f, high_f]
         mask = jnp.concatenate(masks, 0).astype(BF16)
         prefix = lax.dot_general(mask, before, ROWS, preferred_element_type=F32)
         total = lax.dot_general(mask, ones, ROWS, preferred_element_type=F32)
@@ -311,105 +374,13 @@
             dest[(j * 9 + c) * 8 : (j * 9 + c) * 8 + 8, :] = spot
             sizes = (low_n + mid_n + high_n, low_n, mid_n, high_n)
             for size, usual in zip(sizes, USUAL[kind(c)]):
-                over = jnp.maximum(over, size - usual)
+                excess = size - usual
+                if c == 4:
+                    excess = jnp.max(excess, 0, keepdims=True)
+                over = jnp.maximum(over, excess)
         count_v[8:16, j * 128 : j * 128 + 128] = over.astype(jnp.int32)
-    copy = pltpu.make_async_copy(count_v, count_s, copy_sem)
+    copy = pltpu.make_async_copy(count_v, count_s, copy_sem.at[0])
     copy.start()
-    copy.wait()
-
-    for j in range(2):
-
-        def count(c, t, k):
-            return count_s[0, j * 256 + (c * 3 + t) * 8 + k]
-
-        def gather_level(k, offset, sizes):
-            rise = CELL_SIDE * k.astype(F32) - 20.0
-            for c in range(9):
-                di, dj = c // 3 - 1, c % 3 - 1
-                base = ((1 + di) * 4 + 1 + j + dj) * 64
-                value = ext[pl.ds(base + k, 8, stride=8), :]
-                shift = jnp.where(
-                    sub == 0,
-                    CELL_SIDE * di,
-                    jnp.where(sub == 1, CELL_SIDE * dj, jnp.where(sub == 2, rise, 0.0)),
-                )
-                spot = dest[pl.ds((j * 9 + c) * 8 + k, 1), :]
-                rows = sizes[kind(c)][0]
-                picked[c, 0:rows, :] = lax.dot_general(
-                    one_hot(rows, spot),
-                    keyed(value + shift, sub),
-                    LANES,
-                    preferred_element_type=F32,
-                )
-            for t in range(3):
-                if t == 2:
-                    bounds[0, k] = offset
-                for c in range(9):
-                    start = 0 if t == 0 else count(c, 0, k)
-                    if t == 2:
-                        start = start + count(c, 1, k)
-                    length = sizes[kind(c)][1 + t]
-                    packed[pl.ds(offset, length), :] = picked[c, pl.ds(start, length), :]
-                    offset = offset + count(c, t, k)
-                if t == 0:
-                    bounds[1, k] = offset
-            return offset
-
-        def level(k, offset):
-            return lax.cond(
-                count_s[8 + k, j * 128] > 0,
-                lambda: gather_level(k, offset, {t: (128,) * 4 for t in range(3)}),
-                lambda: gather_level(k, offset, USUAL),
-            )
-
-        end = lax.fori_loop(0, 8, level, jnp.int32(0))
-        lane = lax.broadcasted_iota(jnp.int32, (64, KEYS), 1)
-        packed[pl.ds(end, 64), :] = jnp.where((lane >= 24) & (lane < 27), 1.0, 0.0)
-        bounds[1, 8] = end
-
-        def cell(k, _):
-            rise = CELL_SIDE * k.astype(F32) - 20.0
-            base = (5 + j) * 64
-            own = [ext[pl.ds(base + 8 * t + k, 1), :] for t in range(7)]
-            own[2] = own[2] + rise
-            own_table(own, sub, table)
-            first = jnp.where(k == 0, 0, bounds[0, jnp.maximum(k - 1, 0)])
-            first = (first // 8) * 8
-            last = bounds[1, k + 1]
-
-            def fill(i, pairs):
-                at = pl.multiple_of(first + i * CHUNK, 8)
-                pairs[...] = lax.dot_general(
-                    packed[pl.ds(at, CHUNK), :].astype(BF16),
-                    table[...],
-                    ROWS,
-                    preferred_element_type=F32,
-                )
-
-            def use(pairs, acc):
-                for g in range(CHUNK // 8):
-                    pair = [
-                        pairs[g * 8 : g * 8 + 8, t * 128 : t * 128 + 128] for t in range(TERMS)
-                    ]
-                    acc = pair_sums(pair, acc)
-                return acc
-
-            def chunks(i, acc):
-                fill(2 * i + 1, pairs_b)
-                acc = use(pairs_a, acc)
-                fill(2 * i + 2, pairs_a)
-                return use(pairs_b, acc)
-
-            fill(0, pairs_a)
-            zero = jnp.zeros((8, 128), F32)
-            sums = lax.fori_loop(
-                0, (last - first + 2 * CHUNK - 1) // (2 * CHUNK), chunks, (zero, zero, zero)
-            )
-            for t in range(3):
-                force[pl.ds((j * 8 + t) * 8 + k, 1), :] = jnp.sum(sums[t], 0, keepdims=True)
-            return 0
-
-        lax.fori_loop(0, 8, cell, 0)
 
     angle = jnp.full((8, 128), phase[0].astype(F32) * (2.0 * math.pi / PHASES), F32)
     cos_b, sin_b = jnp.cos(angle), jnp.sin(angle)
@@ -419,7 +390,7 @@
     shaft_id = lax.axis_index("shaft").astype(F32)
     lat_id = (lax.axis_index("lat") * 2).astype(F32)
     up_id = sub.astype(F32)
-    terms = []
+    blade = []
     for j in range(2):
         base = (5 + j) * 64
         x, y, z = (ext[base + 8 * t : base + 8 * t + 8, :] for t in range(3))
@@ -433,26 +404,11 @@
         window = jnp.maximum(radial * (reach - radial), 0.0) * (4.0 / (reach * reach))
         gate = jnp.maximum(jnp.cos(x * (2.0 * math.pi / (2.0 * CELL_SIDE))), 0.0)
         size = BLADE_STIFFNESS * depth * window * gate
-        fx, fy, fz = (force[(j * 8 + t) * 8 : (j * 8 + t) * 8 + 8, :] for t in range(3))
-        fy, fz = fy + size * cos_b, fz + size * sin_b
-        ox, oy, oz = (off[t, 0, j] for t in range(3))
-        six = [fx, fy, fz, oy * fz - oz * fy, oz * fx - ox * fz, ox * fy - oy * fx]
-        for t in range(8):
-            force[(j * 8 + t) * 8 : (j * 8 + t) * 8 + 8, :] = (
-                six[t] if t < 6 else jnp.zeros((8, 128), F32)
-            )
-        for k in range(8):
-            terms.append(rows3(force[pl.ds(j * 64 + k, 8, stride=8), :]))
-    sums = lax.dot_general(
-        jnp.concatenate(terms, 1), hot_piece[...], LANES, preferred_element_type=F32
-    )
-    sums = sum3(
-        lax.dot_general(rows3(sum3(sums)), hot_clump[...], LANES, preferred_element_type=F32)
-    )
+        blade.append(size)
+
+    loads[0].wait()
+    loads[1].wait()
     n_clump = part.shape[-1]
-    for c in range(9):
-        part[c] = sums[:, c * n_clump : (c + 1) * n_clump]
-
     cos_z, cos_y, cos_x = (jnp.cos(angles[t, 0]) for t in range(3))
     sin_z, sin_y, sin_x = (jnp.sin(angles[t, 0]) for t in range(3))
     rotation = [
@@ -473,6 +429,134 @@
             rotation[a][i] * inertia[i, 0] * rotation[b][i] for i in range(3)
         )
     turning[6:8, :] = jnp.zeros((2, n_clump), F32)
+    copy.wait()
+
+    lane = lax.broadcasted_iota(jnp.int32, (64, KEYS), 1)
+    inert = jnp.where((lane >= 24) & (lane < 27), 1.0, 0.0)
+    for j in range(2):
+
+        def count(c, t, k):
+            return count_s[0, j * 256 + (c * 3 + t) * 8 + k]
+
+        def pick(c, k, rows, into):
+            di, dj = c // 3 - 1, c % 3 - 1
+            base = ((1 + di) * 4 + 1 + j + dj) * 64
+            rise = CELL_SIDE * k.astype(F32) - 20.0
+            shift = jnp.where(
+                sub == 0,
+                CELL_SIDE * di,
+                jnp.where(sub == 1, CELL_SIDE * dj, jnp.where(sub == 2, rise, 0.0)),
+            )
+            value = ext[pl.ds(base + k, 8, stride=8), :] + shift
+            spot = dest[pl.ds((j * 9 + c) * 8 + k, 1), :]
+            into[0:rows, :] = lax.dot_general(
+                one_hot(rows, spot), keyed(value, sub), LANES, preferred_element_type=F32
+            )
+
+        def pick_own(k, _):
+            pick(4, k, 128, picked_own.at[k])
+            return 0
+
+        lax.fori_loop(0, 8, pick_own, 0)
+
+        def gather_level(k, offset, sizes):
+            sides = [c for c in range(9) if c != 4]
+            for c in sides:
+                pick(c, k, sizes[kind(c)][0], picked.at[c])
+            for t in range(3):
+                start_of_part = offset
+                if t == 2:
+                    bounds[0, k] = offset
+                for c in sides:
+                    start = 0 if t == 0 else count(c, 0, k)
+                    if t == 2:
+                        start = start + count(c, 1, k)
+                    length = sizes[kind(c)][1 + t]
+                    packed[pl.ds(offset, length), :] = picked[c, pl.ds(start, length), :]
+                    offset = offset + count(c, t, k)
+                if t == 0:
+                    bounds[1, k] = offset
+                if t == 1:
+                    packed[pl.ds(offset, 64), :] = inert
+                    offset = jnp.maximum(offset, start_of_part + 64)
+                    below, above = jnp.maximum(k - 1, 0), jnp.minimum(k + 1, 7)
+                    length = sizes[0][1]
+                    start = count(4, 0, below)
+                    packed[pl.ds(offset, length), :] = picked_own[below, pl.ds(start, length), :]
+                    offset = offset + jnp.where(k > 0, count(4, 2, below), 0)
+                    packed[pl.ds(offset, length), :] = picked_own[above, pl.ds(0, length), :]
+                    offset = offset + jnp.where(k < 7, count(4, 0, above), 0)
+                    packed[pl.ds(offset, 8), :] = inert[0:8]
+                    offset = (offset + 7) // 8 * 8
+            return offset
+
+        def level(k, offset):
+            return lax.cond(
+                count_s[8 + k, j * 128] > 0,
+                lambda: gather_level(k, offset, {t: (128,) * 4 for t in range(3)}),
+                lambda: gather_level(k, offset, USUAL),
+            )
+
+        end = lax.fori_loop(0, 8, level, jnp.int32(0))
+        packed[pl.ds(end, 64), :] = inert
+        bounds[1, 8] = end
+
+        def cell(k, _):
+            rise = CELL_SIDE * k.astype(F32) - 20.0
+            base = (5 + j) * 64
+            own = [ext[pl.ds(base + 8 * t + k, 1), :] for t in range(7)]
+            own[2] = own[2] + rise
+            own_table(own, sub, table)
+            first = jnp.where(k == 0, 0, bounds[0, jnp.maximum(k - 1, 0)])
+            last = bounds[1, k + 1]
+
+            def rows(i):
+                return packed[pl.ds(pl.multiple_of(first + i * CHUNK, 8), CHUNK), :]
+
+            def chunks(i, acc):
+                acc = use(pairs_a, acc)
+                fill(rows(2 * i + 2), table, pairs_a)
+                acc = use(pairs_b, acc)
+                fill(rows(2 * i + 3), table, pairs_b)
+                return acc
+
+            fill(rows(0), table, pairs_a)
+            fill(rows(1), table, pairs_b)
+            zero = jnp.zeros((8, 128), F32)
+            sums = lax.fori_loop(
+                0, (last - first + 2 * CHUNK - 1) // (2 * CHUNK), chunks, (zero, zero, zero)
+            )
+            for t in range(3):
+                force[pl.ds((j * 8 + t) * 8 + k, 1), :] = jnp.sum(sums[t], 0, keepdims=True)
+            return 0
+
+        lax.fori_loop(0, 8, cell, 0)
+
+    loads[2].wait()
+    terms = []
+    for j in range(2):
+        fx, fy, fz = (
+            force[(j * 8 + t) * 8 : (j * 8 + t) * 8 + 8, :]
+            + inside[(j * 8 + t) * 8 : (j * 8 + t) * 8 + 8, :]
+            for t in range(3)
+        )
+        fy, fz = fy + blade[j] * cos_b, fz + blade[j] * sin_b
+        ox, oy, oz = (off[t, 0, j] for t in range(3))
+        six = [fx, fy, fz, oy * fz - oz * fy, oz * fx - ox * fz, ox * fy - oy * fx]
+        for t in range(8):
+            force[(j * 8 + t) * 8 : (j * 8 + t) * 8 + 8, :] = (
+                six[t] if t < 6 else jnp.zeros((8, 128), F32)
+            )
+        for k in range(8):
+            terms.append(rows3(force[pl.ds(j * 64 + k, 8, stride=8), :]))
+    sums = lax.dot_general(
+        jnp.concatenate(terms, 1), hot_piece[...], LANES, preferred_element_type=F32
+    )
+    sums = sum3(
+        lax.dot_general(rows3(sum3(sums)), hot_clump[...], LANES, preferred_element_type=F32)
+    )
+    for c in range(9):
+        part[c] = sums[:, c * n_clump : (c + 1) * n_clump]
 
 
 def finish_kernel(
@@ -481,22 +565,40 @@
     part_any,
     part,
     turning,
+    hot_piece,
+    hot_clump,
+    centre_hbm,
+    motion_hbm,
+    inverse_mass_hbm,
+    off_hbm,
+    clump_out,
+    sphere_out,
     centre,
     motion,
     inverse_mass,
     off,
-    hot_piece,
-    hot_clump,
-    clump_out,
-    sphere_out,
     got,
     table,
     pose,
     send_sem,
     recv_sem,
+    load_sem,
 ):
     place = Place(n_shaft, n_lat)
     n_clump = part.shape[-1]
+    loads = [
+        pltpu.make_async_copy(src, dst, load_sem.at[t])
+        for t, (src, dst) in enumerate(
+            (
+                (centre_hbm, centre),
+                (motion_hbm, motion),
+                (inverse_mass_hbm, inverse_mass),
+                (off_hbm, off),
+            )
+        )
+    ]
+    for load in loads:
+        load.start()
 
     def sums_copy(ds, dl, slot):
         c = (ds + 1) * 3 + dl + 1
@@ -538,6 +640,8 @@
 
     clear(0, 0)
     clear(n_lat - 1, 2)
+    for load in loads:
+        load.wait()
     place.lateral(
         lambda dl: around(lambda ds, d: sums_copy(ds, d, 8 - (ds + 1) * 3 - d - 1).wait_recv(), dl)
     )
@@ -596,7 +700,9 @@
     )
 
 
-def contact_call(lat_cells, blade_phase, ext, off, hot_piece, hot_clump, angles, inertia, **extra):
+def contact_call(
+    lat_cells, blade_phase, ext, hot_piece, hot_clump, inside, off, angles, inertia, **extra
+):
     n_clump = angles.shape[-1]
     return pl.pallas_call(
         functools.partial(contact_kernel, lat_cells),
@@ -604,25 +710,29 @@
             jax.ShapeDtypeStruct((9, 8, n_clump), F32),
             jax.ShapeDtypeStruct((8, n_clump), F32),
         ),
-        in_specs=[SMEM] + [VMEM] * 6,
+        in_specs=[SMEM] + [VMEM] * 4 + [HBM] * 3,
         out_specs=(VMEM, VMEM),
         scratch_shapes=[
+            pltpu.VMEM(off.shape, F32),
+            pltpu.VMEM(angles.shape, F32),
+            pltpu.VMEM(inertia.shape, F32),
             pltpu.VMEM((144, 128), jnp.int32),
             pltpu.VMEM((16, 512), jnp.int32),
             pltpu.SMEM((16, 512), jnp.int32),
             pltpu.SMEM((2, 16), jnp.int32),
             pltpu.VMEM((9, 256, KEYS), F32),
-            pltpu.VMEM((9 * 1024 + 256, KEYS), F32),
+            pltpu.VMEM((8, 256, KEYS), F32),
+            pltpu.VMEM((9 * 1024 + 8 * 72 + 256, KEYS), F32),
             pltpu.VMEM((KEYS, TERMS * 128), BF16),
             pltpu.VMEM((CHUNK, TERMS * 128), F32),
             pltpu.VMEM((CHUNK, TERMS * 128), F32),
             pltpu.VMEM((128, 128), F32),
-            pltpu.SemaphoreType.DMA,
+            pltpu.SemaphoreType.DMA((4,)),
         ],
         compiler_params=pltpu.CompilerParams(vmem_limit_bytes=20 << 20),
         name="contact",
         **extra,
-    )(blade_phase, ext, off, hot_piece, hot_clump, angles, inertia)
+    )(blade_phase, ext, hot_piece, hot_clump, inside, off, angles, inertia)
 
 
 def on_device(
@@ -643,19 +753,46 @@
     clump_inverse_inertia,
 ):
     n_piece, n_clump = piece_route.shape[-1], clump_angles.shape[-1]
-    ext, hot_piece, hot_clump = pl.pallas_call(
+    sphere_position, sphere_velocity, sphere_radius, sphere_piece, piece_route, piece_clump = (
+        pltpu.with_memory_space_constraint(v, pltpu.HBM)
+        for v in (
+            sphere_position,
+            sphere_velocity,
+            sphere_radius,
+            sphere_piece,
+            piece_route,
+            piece_clump,
+        )
+    )
+    sphere_offset, clump_centre, clump_motion = (
+        pltpu.with_memory_space_constraint(v, pltpu.HBM)
+        for v in (sphere_offset, clump_centre, clump_motion)
+    )
+    clump_angles, clump_inverse_mass, clump_inverse_inertia = (
+        pltpu.with_memory_space_constraint(v, pltpu.HBM)
+        for v in (clump_angles, clump_inverse_mass, clump_inverse_inertia)
+    )
+    ext, hot_piece, hot_clump, inside = pl.pallas_call(
         functools.partial(halo_kernel, n_shaft, n_lat),
         out_shape=(
             jax.ShapeDtypeStruct((3, 4, 8, 8, 128), F32),
             jax.ShapeDtypeStruct((n_piece, 2048), BF16),
             jax.ShapeDtypeStruct((9 * n_clump, n_piece), BF16),
+            jax.ShapeDtypeStruct((128, 128), F32),
         ),
-        in_specs=[ANY] * 3 + [VMEM] * 3,
-        out_specs=(VMEM,) * 3,
+        in_specs=[HBM] * 6,
+        out_specs=(VMEM,) * 4,
         scratch_shapes=[
+            pltpu.VMEM(sphere_piece.shape, jnp.int32),
+            pltpu.VMEM(piece_route.shape, jnp.int32),
+            pltpu.VMEM(piece_clump.shape, jnp.int32),
+            pltpu.VMEM((KEYS, TERMS * 128), BF16),
+            pltpu.VMEM((CHUNK, TERMS * 128), F32),
+            pltpu.VMEM((CHUNK, TERMS * 128), F32),
             pltpu.SemaphoreType.DMA((3, 4, 3)),
             pltpu.SemaphoreType.DMA((3, 4, 3)),
             pltpu.SemaphoreType.DMA((2, 3)),
+            pltpu.SemaphoreType.DMA((3,)),
         ],
         compiler_params=pltpu.CompilerParams(
             collective_id=0, has_side_effects=True, vmem_limit_bytes=16 << 20
@@ -673,9 +810,10 @@
         2 * n_lat,
         blade_phase,
         ext.reshape(768, 128),
-        sphere_offset,
         hot_piece,
         hot_clump,
+        inside,
+        sphere_offset,
         clump_angles,
         clump_inverse_inertia,
     )
@@ -685,14 +823,19 @@
             jax.ShapeDtypeStruct((9, 1, 1, n_clump), F32),
             jax.ShapeDtypeStruct((6, 1, 2, 8, 128), F32),
         ),
-        in_specs=[ANY] + [VMEM] * 8,
+        in_specs=[VMEM] * 5 + [HBM] * 4,
         out_specs=(VMEM, VMEM),
         scratch_shapes=[
+            pltpu.VMEM(clump_centre.shape, F32),
+            pltpu.VMEM(clump_motion.shape, F32),
+            pltpu.VMEM(clump_inverse_mass.shape, F32),
+            pltpu.VMEM(sphere_offset.shape, F32),
             pltpu.VMEM((9, 8, n_clump), F32),
             pltpu.VMEM((9, 8, n_clump), F32),
             pltpu.VMEM((128, 128), F32),
             pltpu.SemaphoreType.DMA((2, 9)),
             pltpu.SemaphoreType.DMA((2, 9)),
+            pltpu.SemaphoreType.DMA((4,)),
         ],
         compiler_params=pltpu.CompilerParams(
             collective_id=1, has_side_effects=True, vmem_limit_bytes=16 << 20
@@ -702,12 +845,12 @@
         part,
         part,
         turning,
+        hot_piece,
+        hot_clump,
         clump_centre,
         clump_motion,
         clump_inverse_mass,
         sphere_offset,
-        hot_piece,
-        hot_clump,
     )
 
 

time: 77 us -> 65 us (0.84); the launches traced: 76.1 us -> 66.3 us
  local copies, waits for them, and re-layouts: 7.55 us -> 1.22 us
  Pallas kernels: 67.1 us -> 63.8 us
    pallas_call x1, Pallas kernels: 33.8 us -> 26.8 us  [contact_call(): pl.pallas_call(functools.partial(contact_kernel, lat_cells), out_shape=(j...]
    pallas_call x1, Pallas kernels: 12 us -> 18.3 us  [on_device(): pl.pallas_call(functools.partial(halo_kernel, n_shaft, n_lat), out_shape=...]
    unnamed x26 -> x2, local copies, waits for them, and re-layouts: 7.55 us -> 1.22 us
    pallas_call x1, Pallas kernels: 21.4 us -> 18.6 us  [on_device(): pl.pallas_call(functools.partial(finish_kernel, n_shaft, n_lat), out_shap...]
where the time goes in v3:
time: 65 us; the launch traced here: 66.3 us
  Pallas kernels  63.8 us (98%)
  between operations  1.3 us (2%)
  local copies, waits for them, and re-layouts  1.22 us (2%)
    pallas_call x1, Pallas kernels, contact_call(): pl.pallas_call(functools.partial(contact_kernel, lat_cells), out_shape=(j...  26.8 us
    pallas_call x1, Pallas kernels, on_device(): pl.pallas_call(functools.partial(finish_kernel, n_shaft, n_lat), out_shap...  18.6 us
    pallas_call x1, Pallas kernels, on_device(): pl.pallas_call(functools.partial(halo_kernel, n_shaft, n_lat), out_shape=...  18.3 us

profile of v3, /device:TPU:1, one launch (start us, length us, event | category | flops | bytes accessed | tf_op | source)
XLA Modules:
  0.0 66.3 jit_solution(16930388653691486165)
XLA Ops:
  1.3 18.3 %halo.1 = (f32[3,4,8,8,128]{4,3,2,1,0:T(8,128)S(1)}, bf16[512,2048]{1,0:T(8,128)(2,1)S(1)}, bf16[2304,512]{1,0:T(8,128)(2,1)S(1)}, f32[128,128]{1,0:T(8,128)S(1)}) custom-call(f32[3,1,2,8,128]{4,3,2,1,0:T(8,128)} %pos.1, f32[3,1,2,8,128]{4,3,2,1,0:T(8,128)} %vel.1, f32[1,2,8,128]{3,2,1,0:T(8,128)} %rad.1, s32[1,1,2048]{2,1,0:T(1,128)} %piece_hbm.1, ...), custom_call_target="tpu_custom_call" | custom-call | tf_op jit(solution)/shard_map/halo/pallas_call | solution.py:775
  19.6 26.8 %contact.1 = (f32[9,8,256]{2,1,0:T(8,128)S(1)}, f32[8,256]{1,0:T(8,128)S(1)}) custom-call(s32[1]{0:T(128)S(6)} %copy.17.phase, f32[768,128]{1,0:T(8,128)S(1)} %bitcast.1, bf16[512,2048]{1,0:T(8,128)(2,1)S(1)} %get-tuple-element.9.hot_piece, bf16[2304,512]{1,0:T(8,128)(2,1)S(1)} %get-tuple-element.10.hot_clump, f32[128,128]{1,0:T(8,128)S(1)} %get-tuple-element.11.inside, ...), custom_call_target="tpu_custom_call" | custom-call | tf_op jit(solution)/shard_map/contact/pallas_call | solution.py:707
  46.5 18.6 %finish.1 = (f32[9,1,1,256]{3,2,1,0:T(1,128)S(1)}, f32[6,1,2,8,128]{4,3,2,1,0:T(8,128)S(1)}) custom-call(f32[9,8,256]{2,1,0:T(8,128)S(1)} %get-tuple-element.12.part_any.part, f32[9,8,256]{2,1,0:T(8,128)S(1)} %get-tuple-element.12.part_any.part, f32[8,256]{1,0:T(8,128)S(1)} %get-tuple-element.13.turning, bf16[512,2048]{1,0:T(8,128)(2,1)S(1)} %get-tuple-element.9.hot_piece, ...), custom_call_target="tpu_custom_call" | custom-call | tf_op jit(solution)/shard_map/finish/pallas_call | solution.py:820
  65.1 0.6 copy.18
  65.7 0.6 copy.19

commit v4 on v3

--- a/solution.py
+++ b/solution.py
@@ -15,8 +15,8 @@
 TIME_STEP = 0.5
 GRAVITY = 0.5
 
-REACH = 1.2001
-CHUNK = 32
+REACH = 0.6001
+CHUNK = 64
 F32 = jnp.float32
 BF16 = jnp.bfloat16
 MESH = pl.DeviceIdType.MESH
@@ -65,7 +65,7 @@
         pl.when(self.l > 0)(lambda: act(-1))
         pl.when(self.l < self.n_lat - 1)(lambda: act(1))
 
-    def barrier(self):
+    def greet(self):
         sem = pltpu.get_barrier_semaphore()
 
         def signal(dl):
@@ -76,6 +76,9 @@
                     )
 
         self.lateral(signal)
+
+    def meet(self):
+        sem = pltpu.get_barrier_semaphore()
         edge = jnp.logical_or(self.l == 0, self.l == self.n_lat - 1)
         pl.semaphore_wait(sem, jnp.where(edge, 5, 8))
 
@@ -93,12 +96,10 @@
     hot_piece,
     hot_clump,
     inside,
+    tables,
     piece,
     route,
     clump,
-    table,
-    pairs_a,
-    pairs_b,
     send_sem,
     recv_sem,
     own_sem,
@@ -156,7 +157,8 @@
     ]
     for c in own:
         c.start()
-    place.barrier()
+    place.greet()
+    place.meet()
     place.lateral(lambda dl: [c.start() for c in outgoing(dl)] and None)
     ext[:, :, 7] = jnp.zeros((3, 4, 8, 128), F32)
 
@@ -177,15 +179,14 @@
     def cell(m, _):
         j, k = m // 8, m % 8
         mine = [ext[1, 1 + j, t, pl.ds(k, 1), :] for t in range(7)]
-        own_table(mine, sub, table)
+        mine[2] = mine[2] + (CELL_SIDE * k.astype(F32) - 20.0)
+        own_table(mine, sub, tables.at[m])
         value = jnp.concatenate(mine + [mine[6]], 0)
         rows = lax.dot_general(every, keyed(value, sub), LANES, preferred_element_type=F32)
         zero = jnp.zeros((8, 128), F32)
         acc = (zero, zero, zero)
-        for i in range(128 // CHUNK):
-            pairs = (pairs_a, pairs_b)[i % 2]
-            fill(rows[i * CHUNK : (i + 1) * CHUNK], table, pairs)
-            acc = use(pairs, acc)
+        for i in range(0, 128, CHUNK):
+            acc = add_pairs(rows[i : i + CHUNK], tables.at[m], acc)
         for t in range(3):
             inside[pl.ds((j * 8 + t) * 8 + k, 1), :] = jnp.sum(acc[t], 0, keepdims=True)
         return 0
@@ -278,17 +279,10 @@
     )
 
 
-def fill(rows, table, pairs):
-    pairs[...] = lax.dot_general(
-        rows.astype(BF16), table[...], ROWS, preferred_element_type=F32
-    )
-
-
-def use(pairs, acc):
-    for g in range(CHUNK // 8):
-        acc = pair_sums(
-            [pairs[g * 8 : g * 8 + 8, t * 128 : t * 128 + 128] for t in range(TERMS)], acc
-        )
+def add_pairs(rows, table, acc):
+    pairs = lax.dot_general(rows.astype(BF16), table[...], ROWS, preferred_element_type=F32)
+    for g in range(0, CHUNK, 8):
+        acc = pair_sums([pairs[g : g + 8, t * 128 : t * 128 + 128] for t in range(TERMS)], acc)
     return acc
 
 
@@ -296,13 +290,12 @@
     lat_cells,
     phase,
     ext,
-    hot_piece,
-    hot_clump,
     inside,
+    tables,
     off_hbm,
     angles_hbm,
     inertia_hbm,
-    part,
+    force,
     turning,
     off,
     angles,
@@ -312,12 +305,7 @@
     count_s,
     bounds,
     picked,
-    picked_own,
     packed,
-    table,
-    pairs_a,
-    pairs_b,
-    force,
     copy_sem,
 ):
     loads = [
@@ -343,12 +331,15 @@
             di, dj = c // 3 - 1, c % 3 - 1
             base = ((1 + di) * 4 + 1 + j + dj) * 64
             x, y, z = (ext[base + 8 * t : base + 8 * t + 8, :] for t in range(3))
-            keep = ext[base + 48 : base + 56, :] > 0.0
-            if di:
-                keep &= (x < REACH) if di > 0 else (x > CELL_SIDE - REACH)
-            if dj:
-                keep &= (y < REACH) if dj > 0 else (y > CELL_SIDE - REACH)
-            low, high = z < REACH, z > CELL_SIDE - REACH
+            radius = ext[base + 48 : base + 56, :]
+            keep = radius > 0.0
+            near = radius + REACH
+            away = [v if d > 0 else CELL_SIDE - v for v, d in ((x, di), (y, dj)) if d]
+            if len(away) == 1:
+                keep &= away[0] < near
+            if len(away) == 2:
+                keep &= away[0] * away[0] + away[1] * away[1] < near * near
+            low, high = z < near, CELL_SIDE - z < near
             kept = jnp.where(keep, 1.0, 0.0)
             low_f = jnp.where(low, kept, 0.0)
             high_f = jnp.where(high, kept, 0.0)
@@ -408,7 +399,7 @@
 
     loads[0].wait()
     loads[1].wait()
-    n_clump = part.shape[-1]
+    n_clump = turning.shape[-1]
     cos_z, cos_y, cos_x = (jnp.cos(angles[t, 0]) for t in range(3))
     sin_z, sin_y, sin_x = (jnp.sin(angles[t, 0]) for t in range(3))
     rotation = [
@@ -449,20 +440,21 @@
             )
             value = ext[pl.ds(base + k, 8, stride=8), :] + shift
             spot = dest[pl.ds((j * 9 + c) * 8 + k, 1), :]
-            into[0:rows, :] = lax.dot_general(
+            into[k, 0:rows, :] = lax.dot_general(
                 one_hot(rows, spot), keyed(value, sub), LANES, preferred_element_type=F32
             )
 
-        def pick_own(k, _):
-            pick(4, k, 128, picked_own.at[k])
+        sides = [c for c in range(9) if c != 4]
+
+        def pick_two(i, _):
+            for k in (2 * i, 2 * i + 1):
+                for c in range(9):
+                    pick(c, k, USUAL[kind(c)][0], picked.at[c])
             return 0
 
-        lax.fori_loop(0, 8, pick_own, 0)
+        lax.fori_loop(0, 4, pick_two, 0)
 
         def gather_level(k, offset, sizes):
-            sides = [c for c in range(9) if c != 4]
-            for c in sides:
-                pick(c, k, sizes[kind(c)][0], picked.at[c])
             for t in range(3):
                 start_of_part = offset
                 if t == 2:
@@ -472,7 +464,7 @@
                     if t == 2:
                         start = start + count(c, 1, k)
                     length = sizes[kind(c)][1 + t]
-                    packed[pl.ds(offset, length), :] = picked[c, pl.ds(start, length), :]
+                    packed[pl.ds(offset, length), :] = picked[c, k, pl.ds(start, length), :]
                     offset = offset + count(c, t, k)
                 if t == 0:
                     bounds[1, k] = offset
@@ -482,18 +474,23 @@
                     below, above = jnp.maximum(k - 1, 0), jnp.minimum(k + 1, 7)
                     length = sizes[0][1]
                     start = count(4, 0, below)
-                    packed[pl.ds(offset, length), :] = picked_own[below, pl.ds(start, length), :]
+                    packed[pl.ds(offset, length), :] = picked[4, below, pl.ds(start, length), :]
                     offset = offset + jnp.where(k > 0, count(4, 2, below), 0)
-                    packed[pl.ds(offset, length), :] = picked_own[above, pl.ds(0, length), :]
+                    packed[pl.ds(offset, length), :] = picked[4, above, pl.ds(0, length), :]
                     offset = offset + jnp.where(k < 7, count(4, 0, above), 0)
                     packed[pl.ds(offset, 8), :] = inert[0:8]
                     offset = (offset + 7) // 8 * 8
             return offset
 
+        def gather_all(k, offset):
+            for c in sides:
+                pick(c, k, 128, picked.at[c])
+            return gather_level(k, offset, {t: (128,) * 4 for t in range(3)})
+
         def level(k, offset):
             return lax.cond(
                 count_s[8 + k, j * 128] > 0,
-                lambda: gather_level(k, offset, {t: (128,) * 4 for t in range(3)}),
+                lambda: gather_all(k, offset),
                 lambda: gather_level(k, offset, USUAL),
             )
 
@@ -502,30 +499,16 @@
         bounds[1, 8] = end
 
         def cell(k, _):
-            rise = CELL_SIDE * k.astype(F32) - 20.0
-            base = (5 + j) * 64
-            own = [ext[pl.ds(base + 8 * t + k, 1), :] for t in range(7)]
-            own[2] = own[2] + rise
-            own_table(own, sub, table)
             first = jnp.where(k == 0, 0, bounds[0, jnp.maximum(k - 1, 0)])
             last = bounds[1, k + 1]
-
-            def rows(i):
-                return packed[pl.ds(pl.multiple_of(first + i * CHUNK, 8), CHUNK), :]
-
-            def chunks(i, acc):
-                acc = use(pairs_a, acc)
-                fill(rows(2 * i + 2), table, pairs_a)
-                acc = use(pairs_b, acc)
-                fill(rows(2 * i + 3), table, pairs_b)
-                return acc
-
-            fill(rows(0), table, pairs_a)
-            fill(rows(1), table, pairs_b)
+            table = tables.at[j * 8 + k]
+
+            def chunk(i, acc):
+                at = pl.multiple_of(first + i * CHUNK, 8)
+                return add_pairs(packed[pl.ds(at, CHUNK), :], table, acc)
+
             zero = jnp.zeros((8, 128), F32)
-            sums = lax.fori_loop(
-                0, (last - first + 2 * CHUNK - 1) // (2 * CHUNK), chunks, (zero, zero, zero)
-            )
+            sums = lax.fori_loop(0, (last - first + CHUNK - 1) // CHUNK, chunk, (zero, zero, zero))
             for t in range(3):
                 force[pl.ds((j * 8 + t) * 8 + k, 1), :] = jnp.sum(sums[t], 0, keepdims=True)
             return 0
@@ -533,7 +516,6 @@
         lax.fori_loop(0, 8, cell, 0)
 
     loads[2].wait()
-    terms = []
     for j in range(2):
         fx, fy, fz = (
             force[(j * 8 + t) * 8 : (j * 8 + t) * 8 + 8, :]
@@ -547,55 +529,32 @@
             force[(j * 8 + t) * 8 : (j * 8 + t) * 8 + 8, :] = (
                 six[t] if t < 6 else jnp.zeros((8, 128), F32)
             )
-        for k in range(8):
-            terms.append(rows3(force[pl.ds(j * 64 + k, 8, stride=8), :]))
-    sums = lax.dot_general(
-        jnp.concatenate(terms, 1), hot_piece[...], LANES, preferred_element_type=F32
-    )
-    sums = sum3(
-        lax.dot_general(rows3(sum3(sums)), hot_clump[...], LANES, preferred_element_type=F32)
-    )
-    for c in range(9):
-        part[c] = sums[:, c * n_clump : (c + 1) * n_clump]
-
-
-def finish_kernel(
+
+
+def exchange_kernel(
     n_shaft,
     n_lat,
-    part_any,
-    part,
-    turning,
+    force,
     hot_piece,
     hot_clump,
-    centre_hbm,
+    turning,
     motion_hbm,
     inverse_mass_hbm,
-    off_hbm,
-    clump_out,
-    sphere_out,
-    centre,
+    table,
     motion,
     inverse_mass,
-    off,
+    part,
     got,
-    table,
-    pose,
     send_sem,
     recv_sem,
     load_sem,
 ):
     place = Place(n_shaft, n_lat)
-    n_clump = part.shape[-1]
+    n_clump = turning.shape[-1]
+    place.greet()
     loads = [
-        pltpu.make_async_copy(src, dst, load_sem.at[t])
-        for t, (src, dst) in enumerate(
-            (
-                (centre_hbm, centre),
-                (motion_hbm, motion),
-                (inverse_mass_hbm, inverse_mass),
-                (off_hbm, off),
-            )
-        )
+        pltpu.make_async_copy(motion_hbm, motion, load_sem.at[0]),
+        pltpu.make_async_copy(inverse_mass_hbm, inverse_mass, load_sem.at[1]),
     ]
     for load in loads:
         load.start()
@@ -603,7 +562,7 @@
     def sums_copy(ds, dl, slot):
         c = (ds + 1) * 3 + dl + 1
         return pltpu.make_async_remote_copy(
-            src_ref=part_any.at[c],
+            src_ref=part.at[c],
             dst_ref=got.at[slot],
             send_sem=send_sem.at[0, slot],
             recv_sem=recv_sem.at[0, slot],
@@ -626,10 +585,17 @@
             if (ds, dl) != (0, 0):
                 act(ds, dl)
 
-    place.barrier()
-    place.lateral(
-        lambda dl: around(lambda ds, d: sums_copy(ds, d, (ds + 1) * 3 + d + 1).start(), dl)
-    )
+    terms = [
+        rows3(force[pl.ds(j * 64 + k, 8, stride=8), :]) for j in range(2) for k in range(8)
+    ]
+    sums = lax.dot_general(
+        jnp.concatenate(terms, 1), hot_piece[...], LANES, preferred_element_type=F32
+    )
+    sums = sum3(
+        lax.dot_general(rows3(sum3(sums)), hot_clump[...], LANES, preferred_element_type=F32)
+    )
+    for c in range(9):
+        part[c] = sums[:, c * n_clump : (c + 1) * n_clump]
 
     def clear(edge, column):
         @pl.when(place.l == edge)
@@ -640,6 +606,10 @@
 
     clear(0, 0)
     clear(n_lat - 1, 2)
+    place.meet()
+    place.lateral(
+        lambda dl: around(lambda ds, d: sums_copy(ds, d, (ds + 1) * 3 + d + 1).start(), dl)
+    )
     for load in loads:
         load.wait()
     place.lateral(
@@ -659,24 +629,58 @@
         change = sum(turning[order[t][i] : order[t][i] + 1, :] * torque[i] for i in range(3))
         rows.append(motion[3 + t, 0] + change)
     table[4] = jnp.concatenate(rows + [jnp.zeros((2, n_clump), F32)], 0)
-    for t in range(3):
-        clump_out[t, 0] = centre[t, 0] + TIME_STEP * rows[t]
-    for t in range(6):
-        clump_out[3 + t, 0] = rows[t]
     place.lateral(
         lambda dl: around(lambda ds, d: table_copy(ds, d, 8 - (ds + 1) * 3 - d - 1).start(), dl)
     )
     place.lateral(
         lambda dl: around(lambda ds, d: table_copy(ds, d, (ds + 1) * 3 + d + 1).wait_recv(), dl)
     )
+    place.lateral(
+        lambda dl: around(lambda ds, d: sums_copy(ds, d, (ds + 1) * 3 + d + 1).wait_send(), dl)
+    )
+    place.lateral(
+        lambda dl: around(lambda ds, d: table_copy(ds, d, 8 - (ds + 1) * 3 - d - 1).wait_send(), dl)
+    )
+
+
+def spread_kernel(
+    table,
+    hot_piece,
+    hot_clump,
+    centre_hbm,
+    off_hbm,
+    clump_hbm,
+    sphere_hbm,
+    centre,
+    off,
+    clump_out,
+    sphere_out,
+    pose,
+    sem,
+):
+    loads = [
+        pltpu.make_async_copy(centre_hbm, centre, sem.at[0]),
+        pltpu.make_async_copy(off_hbm, off, sem.at[1]),
+    ]
+    for load in loads:
+        load.start()
     tables = jnp.concatenate([rows3(table[c]) for c in range(9)], 1)
     by_piece = lax.dot_general(tables, hot_clump[...], ROWS, preferred_element_type=F32)
     by_piece = by_piece.astype(BF16)
     by_sphere = sum3(
         lax.dot_general(by_piece, hot_piece[...], ROWS, preferred_element_type=F32)
     )
+    loads[0].wait()
+    for t in range(6):
+        row = table[4, t : t + 1, :]
+        if t < 3:
+            clump_out[t, 0] = centre[t, 0] + TIME_STEP * row
+        clump_out[3 + t, 0] = row
+    stores = [pltpu.make_async_copy(clump_out, clump_hbm, sem.at[2])]
+    stores[0].start()
     for m in range(16):
         pose[m * 8 : m * 8 + 8, :] = by_sphere[:, m * 128 : m * 128 + 128]
+    loads[1].wait()
     for j in range(2):
         vx, vy, vz, sx, sy, sz = (
             pose[pl.ds(j * 64 + t, 8, stride=8), :] for t in range(6)
@@ -692,25 +696,25 @@
         sphere_out[3, 0, j] = vx + (sy * tz - sz * ty)
         sphere_out[4, 0, j] = vy + (sz * tx - sx * tz)
         sphere_out[5, 0, j] = vz + (sx * ty - sy * tx)
-    place.lateral(
-        lambda dl: around(lambda ds, d: sums_copy(ds, d, (ds + 1) * 3 + d + 1).wait_send(), dl)
-    )
-    place.lateral(
-        lambda dl: around(lambda ds, d: table_copy(ds, d, 8 - (ds + 1) * 3 - d - 1).wait_send(), dl)
-    )
-
-
-def contact_call(
-    lat_cells, blade_phase, ext, hot_piece, hot_clump, inside, off, angles, inertia, **extra
-):
+        stores.append(
+            pltpu.make_async_copy(
+                sphere_out.at[:, :, pl.ds(j, 1)], sphere_hbm.at[:, :, pl.ds(j, 1)], sem.at[3 + j]
+            )
+        )
+        stores[-1].start()
+    for store in stores:
+        store.wait()
+
+
+def contact_call(lat_cells, blade_phase, ext, inside, tables, off, angles, inertia, **extra):
     n_clump = angles.shape[-1]
     return pl.pallas_call(
         functools.partial(contact_kernel, lat_cells),
         out_shape=(
-            jax.ShapeDtypeStruct((9, 8, n_clump), F32),
+            jax.ShapeDtypeStruct((128, 128), F32),
             jax.ShapeDtypeStruct((8, n_clump), F32),
         ),
-        in_specs=[SMEM] + [VMEM] * 4 + [HBM] * 3,
+        in_specs=[SMEM] + [VMEM] * 3 + [HBM] * 3,
         out_specs=(VMEM, VMEM),
         scratch_shapes=[
             pltpu.VMEM(off.shape, F32),
@@ -720,19 +724,14 @@
             pltpu.VMEM((16, 512), jnp.int32),
             pltpu.SMEM((16, 512), jnp.int32),
             pltpu.SMEM((2, 16), jnp.int32),
-            pltpu.VMEM((9, 256, KEYS), F32),
-            pltpu.VMEM((8, 256, KEYS), F32),
+            pltpu.VMEM((9, 8, 256, KEYS), F32),
             pltpu.VMEM((9 * 1024 + 8 * 72 + 256, KEYS), F32),
-            pltpu.VMEM((KEYS, TERMS * 128), BF16),
-            pltpu.VMEM((CHUNK, TERMS * 128), F32),
-            pltpu.VMEM((CHUNK, TERMS * 128), F32),
-            pltpu.VMEM((128, 128), F32),
             pltpu.SemaphoreType.DMA((4,)),
         ],
-        compiler_params=pltpu.CompilerParams(vmem_limit_bytes=20 << 20),
+        compiler_params=pltpu.CompilerParams(vmem_limit_bytes=24 << 20),
         name="contact",
         **extra,
-    )(blade_phase, ext, hot_piece, hot_clump, inside, off, angles, inertia)
+    )(blade_phase, ext, inside, tables, off, angles, inertia)
 
 
 def on_device(
@@ -772,23 +771,21 @@
         pltpu.with_memory_space_constraint(v, pltpu.HBM)
         for v in (clump_angles, clump_inverse_mass, clump_inverse_inertia)
     )
-    ext, hot_piece, hot_clump, inside = pl.pallas_call(
+    ext, hot_piece, hot_clump, inside, tables = pl.pallas_call(
         functools.partial(halo_kernel, n_shaft, n_lat),
         out_shape=(
             jax.ShapeDtypeStruct((3, 4, 8, 8, 128), F32),
             jax.ShapeDtypeStruct((n_piece, 2048), BF16),
             jax.ShapeDtypeStruct((9 * n_clump, n_piece), BF16),
             jax.ShapeDtypeStruct((128, 128), F32),
+            jax.ShapeDtypeStruct((16, KEYS, TERMS * 128), BF16),
         ),
         in_specs=[HBM] * 6,
-        out_specs=(VMEM,) * 4,
+        out_specs=(VMEM,) * 5,
         scratch_shapes=[
             pltpu.VMEM(sphere_piece.shape, jnp.int32),
             pltpu.VMEM(piece_route.shape, jnp.int32),
             pltpu.VMEM(piece_clump.shape, jnp.int32),
-            pltpu.VMEM((KEYS, TERMS * 128), BF16),
-            pltpu.VMEM((CHUNK, TERMS * 128), F32),
-            pltpu.VMEM((CHUNK, TERMS * 128), F32),
             pltpu.SemaphoreType.DMA((3, 4, 3)),
             pltpu.SemaphoreType.DMA((3, 4, 3)),
             pltpu.SemaphoreType.DMA((2, 3)),
@@ -806,52 +803,54 @@
         piece_route,
         piece_clump,
     )
-    part, turning = contact_call(
+    force, turning = contact_call(
         2 * n_lat,
         blade_phase,
         ext.reshape(768, 128),
-        hot_piece,
-        hot_clump,
         inside,
+        tables,
         sphere_offset,
         clump_angles,
         clump_inverse_inertia,
     )
+    table = pl.pallas_call(
+        functools.partial(exchange_kernel, n_shaft, n_lat),
+        out_shape=jax.ShapeDtypeStruct((9, 8, n_clump), F32),
+        in_specs=[VMEM] * 4 + [HBM] * 2,
+        out_specs=VMEM,
+        scratch_shapes=[
+            pltpu.VMEM(clump_motion.shape, F32),
+            pltpu.VMEM(clump_inverse_mass.shape, F32),
+            pltpu.VMEM((9, 8, n_clump), F32),
+            pltpu.VMEM((9, 8, n_clump), F32),
+            pltpu.SemaphoreType.DMA((2, 9)),
+            pltpu.SemaphoreType.DMA((2, 9)),
+            pltpu.SemaphoreType.DMA((2,)),
+        ],
+        compiler_params=pltpu.CompilerParams(
+            collective_id=1, has_side_effects=True, vmem_limit_bytes=16 << 20
+        ),
+        name="exchange",
+    )(force, hot_piece, hot_clump, turning, clump_motion, clump_inverse_mass)
     return pl.pallas_call(
-        functools.partial(finish_kernel, n_shaft, n_lat),
+        spread_kernel,
         out_shape=(
             jax.ShapeDtypeStruct((9, 1, 1, n_clump), F32),
             jax.ShapeDtypeStruct((6, 1, 2, 8, 128), F32),
         ),
-        in_specs=[VMEM] * 5 + [HBM] * 4,
-        out_specs=(VMEM, VMEM),
+        in_specs=[VMEM] * 3 + [HBM] * 2,
+        out_specs=(HBM, HBM),
         scratch_shapes=[
             pltpu.VMEM(clump_centre.shape, F32),
-            pltpu.VMEM(clump_motion.shape, F32),
-            pltpu.VMEM(clump_inverse_mass.shape, F32),
             pltpu.VMEM(sphere_offset.shape, F32),
-            pltpu.VMEM((9, 8, n_clump), F32),
-            pltpu.VMEM((9, 8, n_clump), F32),
+            pltpu.VMEM((9, 1, 1, n_clump), F32),
+            pltpu.VMEM((6, 1, 2, 8, 128), F32),
             pltpu.VMEM((128, 128), F32),
-            pltpu.SemaphoreType.DMA((2, 9)),
-            pltpu.SemaphoreType.DMA((2, 9)),
-            pltpu.SemaphoreType.DMA((4,)),
+            pltpu.SemaphoreType.DMA((5,)),
         ],
-        compiler_params=pltpu.CompilerParams(
-            collective_id=1, has_side_effects=True, vmem_limit_bytes=16 << 20
-        ),
-        name="finish",
-    )(
-        part,
-        part,
-        turning,
-        hot_piece,
-        hot_clump,
-        clump_centre,
-        clump_motion,
-        clump_inverse_mass,
-        sphere_offset,
-    )
+        compiler_params=pltpu.CompilerParams(vmem_limit_bytes=16 << 20),
+        name="spread",
+    )(table, hot_piece, hot_clump, clump_centre, sphere_offset)
 
 
 def solution(mesh):

time: 65 us -> 62.8 us (0.966); the launches traced: 66.3 us -> 62.1 us
  Pallas kernels: 63.8 us -> 60.8 us
  local copies, waits for them, and re-layouts: 1.22 us -> 0 us
    pallas_call x1, Pallas kernels: 26.8 us -> 22.2 us  [contact_call(): pl.pallas_call(functools.partial(contact_kernel, lat_cells), out_shape=(j...]
    pallas_call x1 -> x2, Pallas kernels: 18.6 us -> 20.5 us  [the longest x1 18.3 us: on_device(): pl.pallas_call(functools.partial(exchange_kernel, n_shaft, n_lat), out_sh...]
    unnamed x2 -> x0, local copies, waits for them, and re-layouts: 1.22 us -> none
where the time goes in v4:
time: 62.8 us; the launch traced here: 62.1 us
  Pallas kernels  60.8 us (97%)
  between operations  1.3 us (2%)
    pallas_call x1, Pallas kernels, contact_call(): pl.pallas_call(functools.partial(contact_kernel, lat_cells), out_shape=(j...  22.2 us
    pallas_call x1, Pallas kernels, on_device(): pl.pallas_call(functools.partial(exchange_kernel, n_shaft, n_lat), out_sh...  18.3 us
    pallas_call x1, Pallas kernels, on_device(): pl.pallas_call(functools.partial(halo_kernel, n_shaft, n_lat), out_shape=...  18 us
    pallas_call x1, Pallas kernels, on_device(): pl.pallas_call(spread_kernel, out_shape=(jax.ShapeDtypeStruct((9, 1, 1, n...  2.24 us

profile of v4, /device:TPU:1, one launch (start us, length us, event | category | flops | bytes accessed | tf_op | source)
XLA Modules:
  0.0 62.1 jit_solution(12815455025740282110)
XLA Ops:
  1.3 18.0 %halo.1 = (f32[3,4,8,8,128]{4,3,2,1,0:T(8,128)S(1)}, bf16[512,2048]{1,0:T(8,128)(2,1)S(1)}, bf16[2304,512]{1,0:T(8,128)(2,1)S(1)}, f32[128,128]{1,0:T(8,128)S(1)}, bf16[16,32,1152]{2,1,0:T(8,128)(2,1)S(1)}) custom-call(f32[3,1,2,8,128]{4,3,2,1,0:T(8,128)} %pos.1, f32[3,1,2,8,128]{4,3,2,1,0:T(8,128)} %vel.1, f32[1,2,8,128]{3,2,1,0:T(8,128)} %rad.1, ...), custom_call_target="tpu_custom_call" | custom-call | tf_op jit(solution)/shard_map/halo/pallas_call | solution.py:774
  19.3 22.2 %contact.1 = (f32[128,128]{1,0:T(8,128)S(1)}, f32[8,256]{1,0:T(8,128)S(1)}) custom-call(s32[1]{0:T(128)S(6)} %copy.15.phase, f32[768,128]{1,0:T(8,128)S(1)} %bitcast.1, f32[128,128]{1,0:T(8,128)S(1)} %get-tuple-element.10.inside, bf16[16,32,1152]{2,1,0:T(8,128)(2,1)S(1)} %get-tuple-element.11.tables, f32[3,1,2,8,128]{4,3,2,1,0:T(8,128)} %off_hbm.3, ...), custom_call_target="tpu_custom_call" | custom-call | tf_op jit(solution)/shard_map/contact/pallas_call | solution.py:711
  41.5 18.3 %exchange.1.table = f32[9,8,256]{2,1,0:T(8,128)S(1)} custom-call(f32[128,128]{1,0:T(8,128)S(1)} %get-tuple-element.12.force, bf16[512,2048]{1,0:T(8,128)(2,1)S(1)} %get-tuple-element.13.hot_piece, bf16[2304,512]{1,0:T(8,128)(2,1)S(1)} %get-tuple-element.14.hot_clump, f32[8,256]{1,0:T(8,128)S(1)} %get-tuple-element.15.turning, f32[6,1,1,256]{3,2,1,0:T(1,128)} %motion_hbm.1, ...), custom_call_target="tpu_custom_call" | custom-call | tf_op jit(solution)/shard_map/exchange/pallas_call | solution.py:816
  59.8 2.2 %spread.1 = (f32[9,1,1,256]{3,2,1,0:T(1,128)}, f32[6,1,2,8,128]{4,3,2,1,0:T(8,128)}) custom-call(f32[9,8,256]{2,1,0:T(8,128)S(1)} %exchange.1.table, bf16[512,2048]{1,0:T(8,128)(2,1)S(1)} %get-tuple-element.13.hot_piece, bf16[2304,512]{1,0:T(8,128)(2,1)S(1)} %get-tuple-element.14.hot_clump, f32[3,1,1,256]{3,2,1,0:T(1,128)} %centre_hbm.1, ...), custom_call_target="tpu_custom_call" | custom-call | tf_op jit(solution)/shard_map/spread/pallas_call | solution.py:835

commit v5 on v4

--- a/solution.py
+++ b/solution.py
@@ -39,7 +39,7 @@
     high = x.astype(BF16).astype(F32)
     rest = x - high
     middle = rest.astype(BF16).astype(F32)
-    return jnp.concatenate([high, middle, rest - middle], 0).astype(BF16)
+    return jnp.concatenate([high, middle, rest - middle], 0)
 
 
 def sum3(x):
@@ -95,6 +95,7 @@
     ext,
     hot_piece,
     hot_clump,
+    route_rows,
     inside,
     tables,
     piece,
@@ -196,11 +197,8 @@
         hot_piece[:, m * 128 : m * 128 + 128] = one_hot(
             hot_piece.shape[0], piece[0, :, m * 128 : m * 128 + 128]
         )
-    n_clump = hot_clump.shape[0] // 9
-    for c in range(9):
-        hot_clump[c * n_clump : (c + 1) * n_clump, :] = one_hot(
-            n_clump, jnp.where(route[0] == c, clump[0], -1)
-        )
+    hot_clump[...] = one_hot(hot_clump.shape[0], clump[0])
+    route_rows[...] = jnp.broadcast_to(route[0], route_rows.shape)
     place.lateral(lambda dl: [c.wait_recv() for c in incoming(dl)] and None)
     place.lateral(lambda dl: [c.wait_send() for c in outgoing(dl)] and None)
 
@@ -365,10 +363,8 @@
             dest[(j * 9 + c) * 8 : (j * 9 + c) * 8 + 8, :] = spot
             sizes = (low_n + mid_n + high_n, low_n, mid_n, high_n)
             for size, usual in zip(sizes, USUAL[kind(c)]):
-                excess = size - usual
-                if c == 4:
-                    excess = jnp.max(excess, 0, keepdims=True)
-                over = jnp.maximum(over, excess)
+                over = jnp.maximum(over, size - usual)
+        over = jnp.broadcast_to(jnp.max(over, 0, keepdims=True), (8, 128))
         count_v[8:16, j * 128 : j * 128 + 128] = over.astype(jnp.int32)
     copy = pltpu.make_async_copy(count_v, count_s, copy_sem.at[0])
     copy.start()
@@ -471,7 +467,7 @@
                 if t == 1:
                     packed[pl.ds(offset, 64), :] = inert
                     offset = jnp.maximum(offset, start_of_part + 64)
-                    below, above = jnp.maximum(k - 1, 0), jnp.minimum(k + 1, 7)
+                    below, above = (k + 7) % 8, (k + 1) % 8
                     length = sizes[0][1]
                     start = count(4, 0, below)
                     packed[pl.ds(offset, length), :] = picked[4, below, pl.ds(start, length), :]
@@ -482,19 +478,21 @@
                     offset = (offset + 7) // 8 * 8
             return offset
 
-        def gather_all(k, offset):
-            for c in sides:
-                pick(c, k, 128, picked.at[c])
-            return gather_level(k, offset, {t: (128,) * 4 for t in range(3)})
-
-        def level(k, offset):
-            return lax.cond(
-                count_s[8 + k, j * 128] > 0,
-                lambda: gather_all(k, offset),
-                lambda: gather_level(k, offset, USUAL),
-            )
-
-        end = lax.fori_loop(0, 8, level, jnp.int32(0))
+        def gather_usual():
+            offset = 0
+            for k in range(8):
+                offset = gather_level(k, offset, USUAL)
+            return offset
+
+        def gather_any():
+            def level(k, offset):
+                for c in sides:
+                    pick(c, k, 128, picked.at[c])
+                return gather_level(k, offset, {t: (128,) * 4 for t in range(3)})
+
+            return lax.fori_loop(0, 8, level, jnp.int32(0))
+
+        end = lax.cond(count_s[8, j * 128] > 0, gather_any, gather_usual)
         packed[pl.ds(end, 64), :] = inert
         bounds[1, 8] = end
 
@@ -537,6 +535,7 @@
     force,
     hot_piece,
     hot_clump,
+    route_rows,
     turning,
     motion_hbm,
     inverse_mass_hbm,
@@ -586,16 +585,19 @@
                 act(ds, dl)
 
     terms = [
-        rows3(force[pl.ds(j * 64 + k, 8, stride=8), :]) for j in range(2) for k in range(8)
+        rows3(force[pl.ds(j * 64 + k, 8, stride=8), :]).astype(BF16) for j in range(2) for k in range(8)
     ]
     sums = lax.dot_general(
         jnp.concatenate(terms, 1), hot_piece[...], LANES, preferred_element_type=F32
     )
-    sums = sum3(
-        lax.dot_general(rows3(sum3(sums)), hot_clump[...], LANES, preferred_element_type=F32)
+    sums = rows3(sum3(sums))
+    route = jnp.concatenate([route_rows[...]] * 3, 0)
+    routed = jnp.concatenate([jnp.where(route == c, sums, 0.0) for c in range(9)], 0)
+    sums = lax.dot_general(
+        routed.astype(BF16), hot_clump[...], LANES, preferred_element_type=F32
     )
     for c in range(9):
-        part[c] = sums[:, c * n_clump : (c + 1) * n_clump]
+        part[c] = sum3(sums[24 * c : 24 * c + 24])
 
     def clear(edge, column):
         @pl.when(place.l == edge)
@@ -647,6 +649,7 @@
     table,
     hot_piece,
     hot_clump,
+    route_rows,
     centre_hbm,
     off_hbm,
     clump_hbm,
@@ -664,11 +667,14 @@
     ]
     for load in loads:
         load.start()
-    tables = jnp.concatenate([rows3(table[c]) for c in range(9)], 1)
-    by_piece = lax.dot_general(tables, hot_clump[...], ROWS, preferred_element_type=F32)
-    by_piece = by_piece.astype(BF16)
+    tables = jnp.concatenate([rows3(table[c]) for c in range(9)], 0).astype(BF16)
+    found = lax.dot_general(tables, hot_clump[...], ROWS, preferred_element_type=F32)
+    route = jnp.concatenate([route_rows[...]] * 3, 0)
+    by_piece = found[0:24]
+    for c in range(1, 9):
+        by_piece = jnp.where(route == c, found[24 * c : 24 * c + 24], by_piece)
     by_sphere = sum3(
-        lax.dot_general(by_piece, hot_piece[...], ROWS, preferred_element_type=F32)
+        lax.dot_general(by_piece.astype(BF16), hot_piece[...], ROWS, preferred_element_type=F32)
     )
     loads[0].wait()
     for t in range(6):
@@ -771,17 +777,18 @@
         pltpu.with_memory_space_constraint(v, pltpu.HBM)
         for v in (clump_angles, clump_inverse_mass, clump_inverse_inertia)
     )
-    ext, hot_piece, hot_clump, inside, tables = pl.pallas_call(
+    ext, hot_piece, hot_clump, route_rows, inside, tables = pl.pallas_call(
         functools.partial(halo_kernel, n_shaft, n_lat),
         out_shape=(
             jax.ShapeDtypeStruct((3, 4, 8, 8, 128), F32),
             jax.ShapeDtypeStruct((n_piece, 2048), BF16),
-            jax.ShapeDtypeStruct((9 * n_clump, n_piece), BF16),
+            jax.ShapeDtypeStruct((n_clump, n_piece), BF16),
+            jax.ShapeDtypeStruct((8, n_piece), jnp.int32),
             jax.ShapeDtypeStruct((128, 128), F32),
             jax.ShapeDtypeStruct((16, KEYS, TERMS * 128), BF16),
         ),
         in_specs=[HBM] * 6,
-        out_specs=(VMEM,) * 5,
+        out_specs=(VMEM,) * 6,
         scratch_shapes=[
             pltpu.VMEM(sphere_piece.shape, jnp.int32),
             pltpu.VMEM(piece_route.shape, jnp.int32),
@@ -816,7 +823,7 @@
     table = pl.pallas_call(
         functools.partial(exchange_kernel, n_shaft, n_lat),
         out_shape=jax.ShapeDtypeStruct((9, 8, n_clump), F32),
-        in_specs=[VMEM] * 4 + [HBM] * 2,
+        in_specs=[VMEM] * 5 + [HBM] * 2,
         out_specs=VMEM,
         scratch_shapes=[
             pltpu.VMEM(clump_motion.shape, F32),
@@ -831,14 +838,14 @@
             collective_id=1, has_side_effects=True, vmem_limit_bytes=16 << 20
         ),
         name="exchange",
-    )(force, hot_piece, hot_clump, turning, clump_motion, clump_inverse_mass)
+    )(force, hot_piece, hot_clump, route_rows, turning, clump_motion, clump_inverse_mass)
     return pl.pallas_call(
         spread_kernel,
         out_shape=(
             jax.ShapeDtypeStruct((9, 1, 1, n_clump), F32),
             jax.ShapeDtypeStruct((6, 1, 2, 8, 128), F32),
         ),
-        in_specs=[VMEM] * 3 + [HBM] * 2,
+        in_specs=[VMEM] * 4 + [HBM] * 2,
         out_specs=(HBM, HBM),
         scratch_shapes=[
             pltpu.VMEM(clump_centre.shape, F32),
@@ -850,7 +857,7 @@
         ],
         compiler_params=pltpu.CompilerParams(vmem_limit_bytes=16 << 20),
         name="spread",
-    )(table, hot_piece, hot_clump, clump_centre, sphere_offset)
+    )(table, hot_piece, hot_clump, route_rows, clump_centre, sphere_offset)
 
 
 def solution(mesh):

time: 62.8 us -> 62.5 us (level)
    pallas_call x1, Pallas kernels: 18.3 us -> 19.1 us  [on_device(): pl.pallas_call(functools.partial(exchange_kernel, n_shaft, n_lat), out_sh...]
where the time goes in v5:
time: 62.5 us; the launch traced here: 62.1 us
  Pallas kernels  60.8 us (97%)
  between operations  1.3 us (2%)
    pallas_call x1, Pallas kernels, contact_call(): pl.pallas_call(functools.partial(contact_kernel, lat_cells), out_shape=(j...  22.1 us
    pallas_call x1, Pallas kernels, on_device(): pl.pallas_call(functools.partial(exchange_kernel, n_shaft, n_lat), out_sh...  19.1 us
    pallas_call x1, Pallas kernels, on_device(): pl.pallas_call(functools.partial(halo_kernel, n_shaft, n_lat), out_shape=...  17.6 us
    pallas_call x1, Pallas kernels, on_device(): pl.pallas_call(spread_kernel, out_shape=(jax.ShapeDtypeStruct((9, 1, 1, n...  1.96 us

profile of v5, /device:TPU:1, one launch (start us, length us, event | category | flops | bytes accessed | tf_op | source)
XLA Modules:
  0.0 62.1 jit_solution(1440301885985643470)
XLA Ops:
  1.3 17.6 %halo.1 = (f32[3,4,8,8,128]{4,3,2,1,0:T(8,128)S(1)}, bf16[512,2048]{1,0:T(8,128)(2,1)S(1)}, bf16[256,512]{1,0:T(8,128)(2,1)S(1)}, s32[8,512]{1,0:T(8,128)S(1)}, ...) custom-call(f32[3,1,2,8,128]{4,3,2,1,0:T(8,128)} %pos.1, f32[3,1,2,8,128]{4,3,2,1,0:T(8,128)} %vel.1, ...), custom_call_target="tpu_custom_call" | custom-call | tf_op jit(solution)/shard_map/halo/pallas_call | solution.py:780
  18.9 22.1 %contact.1 = (f32[128,128]{1,0:T(8,128)S(1)}, f32[8,256]{1,0:T(8,128)S(1)}) custom-call(s32[1]{0:T(128)S(6)} %copy.15.phase, f32[768,128]{1,0:T(8,128)S(1)} %bitcast.1, f32[128,128]{1,0:T(8,128)S(1)} %get-tuple-element.11.inside, bf16[16,32,1152]{2,1,0:T(8,128)(2,1)S(1)} %get-tuple-element.12.tables, f32[3,1,2,8,128]{4,3,2,1,0:T(8,128)} %off_hbm.3, ...), custom_call_target="tpu_custom_call" | custom-call | tf_op jit(solution)/shard_map/contact/pallas_call | solution.py:717
  41.1 19.1 %exchange.1.table = f32[9,8,256]{2,1,0:T(8,128)S(1)} custom-call(f32[128,128]{1,0:T(8,128)S(1)} %get-tuple-element.13.force, bf16[512,2048]{1,0:T(8,128)(2,1)S(1)} %get-tuple-element.14.hot_piece, bf16[256,512]{1,0:T(8,128)(2,1)S(1)} %get-tuple-element.15.hot_clump, s32[8,512]{1,0:T(8,128)S(1)} %get-tuple-element.16.route_rows, ...), custom_call_target="tpu_custom_call" | custom-call | tf_op jit(solution)/shard_map/exchange/pallas_call | solution.py:823
  60.1 2.0 %spread.1 = (f32[9,1,1,256]{3,2,1,0:T(1,128)}, f32[6,1,2,8,128]{4,3,2,1,0:T(8,128)}) custom-call(f32[9,8,256]{2,1,0:T(8,128)S(1)} %exchange.1.table, bf16[512,2048]{1,0:T(8,128)(2,1)S(1)} %get-tuple-element.14.hot_piece, bf16[256,512]{1,0:T(8,128)(2,1)S(1)} %get-tuple-element.15.hot_clump, s32[8,512]{1,0:T(8,128)S(1)} %get-tuple-element.16.route_rows, ...), custom_call_target="tpu_custom_call" | custom-call | tf_op jit(solution)/shard_map/spread/pallas_call | solution.py:842
